TPU v7x, 32 devices: a whole 2x2x4 slice. The times are simulated.
32 devices in a mesh: tile: 8 (over z, y), depth: 4 (over x, core).
Axes of the slice: x: 2, y: 2, z: 4, core: 2. Of those that a mesh axis runs over, the one named last changes fastest.
Arguments:
- volume: bfloat16 [128, 128, 2048], P('tile', 'depth'), may hold values from -4 to 4
Outputs:
- image: float32 [4, 128, 2048], P(None, ('tile', 'depth'))
All inputs are finite; a program needn't handle non-finite values.
Results may differ from a plain program's by a relative error of at most 0.0003.
Values may be sent and summed in bfloat16 or wider, within the bound.
No kernel may reach another device: no remote copies, remote signals or barrier semaphores. Data moves between devices by JAX's collectives and lax.ppermute only.
A program may use at most 64 MiB of HBM per device.

v0:
```python
import jax
import jax.numpy as jnp
from jax import lax
from jax.sharding import PartitionSpec as P

OPACITY = 3.0
LIGHT_X = 0.48
LIGHT_Y = 0.6
LIGHT_Z = 0.64


def padded_2(block, sides, width):
    for axis, dim in sides:
        count = lax.axis_size(axis)
        forward = [(i, i + 1) for i in range(count - 1)]
        backward = [(target, source) for source, target in forward]
        low = lax.ppermute(
            lax.slice_in_dim(block, block.shape[dim] - width, None, axis=dim), axis, forward
        )
        high = lax.ppermute(lax.slice_in_dim(block, 0, width, axis=dim), axis, backward)
        block = jnp.concatenate([low, block, high], axis=dim)
    return block


def partner_2(x, axis, stride):
    return lax.ppermute(x, axis, [(i, i ^ 1 << stride) for i in range(lax.axis_size(axis))])


def brick_image(padded, depth_total):
    field = padded.astype(jnp.float32)
    center = field[1:-1, 1:-1, 1:-1]
    grad_x = 0.5 * (field[2:, 1:-1, 1:-1] - field[:-2, 1:-1, 1:-1])
    grad_z = 0.5 * (field[1:-1, 2:, 1:-1] - field[1:-1, :-2, 1:-1])
    grad_y = 0.5 * (field[1:-1, 1:-1, 2:] - field[1:-1, 1:-1, :-2])
    facing = LIGHT_X * grad_x + LIGHT_Y * grad_y + LIGHT_Z * grad_z
    shade = 0.3 + 0.7 * jnp.abs(facing) / jnp.sqrt(
        1.0 + grad_x * grad_x + grad_y * grad_y + grad_z * grad_z
    )
    squared = center * center
    extinct = OPACITY / depth_total * squared / (1.0 + squared)
    before = jnp.cumsum(extinct, axis=1) - extinct
    weight = jnp.exp(-before) * (1.0 - jnp.exp(-extinct)) * shade
    red = jnp.sum(weight * jax.nn.sigmoid(2.0 * center), axis=1)
    green = jnp.sum(weight * (0.5 * jnp.exp(-squared)), axis=1)
    blue = jnp.sum(weight * jax.nn.sigmoid(-2.0 * center), axis=1)
    passing = jnp.exp(-jnp.sum(extinct, axis=1))
    return jnp.stack([red, green, blue, passing], 0)


def shards(volume):
    depth_count = lax.axis_size("depth")
    cells_x = volume.shape[0]
    rows_y = volume.shape[2]
    pieces = cells_x // depth_count
    depth_total = volume.shape[1] * depth_count
    extended = padded_2(volume, (("tile", 0), ("depth", 1)), 1)
    extended = jnp.pad(extended, ((0, 0), (0, 0), (1, 1)))
    part = brick_image(extended, depth_total)
    levels = depth_count.bit_length() - 1
    buffer = part.reshape((4,) + (2,) * levels + (pieces, rows_y))
    position = lax.axis_index("depth")
    for section in range(levels):
        target = 1 + (levels - 1 - section)
        upper = position // 2**section % 2
        kept = lax.dynamic_slice_in_dim(buffer, upper, 1, target)
        given = lax.dynamic_slice_in_dim(buffer, 1 - upper, 1, target)
        partner = partner_2(given, "depth", section)
        front = jnp.where(upper == 0, kept, partner)
        behind = jnp.where(upper == 0, partner, kept)
        buffer = jnp.concatenate([front[:3] + front[3:4] * behind[:3], front[3:4] * behind[3:4]], 0)
    buffer = buffer.reshape(4, pieces, rows_y)
    colour, passing = (buffer[:3], buffer[3:])
    return jnp.concatenate([colour, 1.0 - passing], 0)


def solution(mesh):
    in_specs = (P("tile", "depth", None),)
    out_specs = P(None, ("tile", "depth"), None)
    return jax.shard_map(shards, mesh=mesh, in_specs=in_specs, out_specs=out_specs, check_vma=False)
```

profile of v0, /device:TPU:4, one launch (start us, length us, event | category | flops | bytes accessed | tf_op | source)
XLA Modules:
  0.0 55.1 jit_solution(271246960970680836)
XLA Ops:
  0.0 2.7 %copy.2 = bf16[16,32,2048]{2,0,1:T(8,128)(2,1)S(1)} copy(bf16[16,32,2048]{2,1,0:T(8,128)(2,1)} %param.1) | data formatting | bytes 4194304 | tf_op args[0]
  2.7 0.4 fusion.16
  3.2 3.4 %collective-permute-start = (bf16[1,32,2048]{2,0,1:T(2,128)(2,1)S(1)}, bf16[1,32,2048]{2,0,1:T(2,128)(2,1)S(1)}, u32[]{:S(2)}, u32[]{:S(2)}) collective-permute-start(bf16[1,32,2048]{2,0,1:T(2,128)(2,1)S(1)} %get-tuple-element.11), channel_id=1, source_target_pairs={{0,4},{4,8},{8,12},{12,16},{16,20},{20,24},{24,28},{1,5},{5,9},{9,... | collective-permute-start | bytes 393224 | tf_op jit(solution)/shard_map/ppermute | solution.py:17
  6.6 2.4 %collective-permute-start.1 = (bf16[1,32,2048]{2,0,1:T(2,128)(2,1)S(1)}, bf16[1,32,2048]{2,0,1:T(2,128)(2,1)S(1)}, u32[]{:S(2)}, u32[]{:S(2)}) collective-permute-start(bf16[1,32,2048]{2,0,1:T(2,128)(2,1)S(1)} %get-tuple-element.12), channel_id=1, source_target_pairs={{4,0},{8,4},{12,8},{16,12},{20,16},{24,20},{28,24},{5,1},{9,5},{13... | collective-permute-start | bytes 393224 | tf_op jit(solution)/shard_map/ppermute | solution.py:20
  9.0 9.7 %collective-permute-done = bf16[1,32,2048]{2,0,1:T(2,128)(2,1)S(1)} collective-permute-done((bf16[1,32,2048]{2,0,1:T(2,128)(2,1)S(1)}, bf16[1,32,2048]{2,0,1:T(2,128)(2,1)S(1)}, u32[]{:S(2)}, u32[]{:S(2)}) %collective-permute-start) | collective-permute-done | bytes 131104 | tf_op jit(solution)/shard_map/ppermute | solution.py:17
  18.7 0.0 collective-permute-done.1
  18.7 0.1 pad_maximum_fusion.3
  18.8 1.3 %collective-permute-start.2 = (bf16[18,1,2048]{2,0,1:T(8,128)(2,1)S(1)}, bf16[18,1,2048]{2,0,1:T(8,128)(2,1)S(1)}, u32[]{:S(2)}, u32[]{:S(2)}) collective-permute-start(bf16[18,1,2048]{2,0,1:T(8,128)(2,1)S(1)} %get-tuple-element.9), channel_id=1, source_target_pairs={{0,1},{1,2},{2,3},{4,5},{5,6},{6,7},{8,9},{9,10},{10,11},{12,13},{... | collective-permute-start | bytes 221192 | tf_op jit(solution)/shard_map/ppermute | solution.py:17
  20.1 1.3 %collective-permute-start.3 = (bf16[18,1,2048]{2,0,1:T(8,128)(2,1)S(1)}, bf16[18,1,2048]{2,0,1:T(8,128)(2,1)S(1)}, u32[]{:S(2)}, u32[]{:S(2)}) collective-permute-start(bf16[18,1,2048]{2,0,1:T(8,128)(2,1)S(1)} %get-tuple-element.10), channel_id=1, source_target_pairs={{1,0},{2,1},{3,2},{5,4},{6,5},{7,6},{9,8},{10,9},{11,10},{13,12},{... | collective-permute-start | bytes 221192 | tf_op jit(solution)/shard_map/ppermute | solution.py:20
  21.4 0.0 collective-permute-done.2
  21.5 3.6 %collective-permute-done.3 = bf16[18,1,2048]{2,0,1:T(8,128)(2,1)S(1)} collective-permute-done((bf16[18,1,2048]{2,0,1:T(8,128)(2,1)S(1)}, bf16[18,1,2048]{2,0,1:T(8,128)(2,1)S(1)}, u32[]{:S(2)}, u32[]{:S(2)}) %collective-permute-start.3) | collective-permute-done | bytes 73760 | tf_op jit(solution)/shard_map/ppermute | solution.py:20
  25.0 5.4 %fusion.1 = f32[18,34,2050]{2,0,1:T(8,128)S(1)} fusion(bf16[18,1,2048]{2,0,1:T(8,128)(2,1)S(1)} %collective-permute-done.3, bf16[18,1,2048]{2,0,1:T(8,128)(2,1)S(1)} %collective-permute-done.2, bf16[1,32,2048]{2,0,1:T(2,128)(2,1)S(1)} %collective-permute-done.1, bf16[16,32,2048]{2,0,1:T(8,128)(2,1)S(1)} %copy.2, bf16[1,32,2048]{2,0,1:T(2,128)(2,1)S(1)} %collective-permute-done), kind=kLoop, calls=%fused_computation.12 | loop fusion | flops 22582800 | bytes 7525152 | tf_op jit(solution)/shard_map/convert_element_type | solution.py:30
  30.5 12.8 %multiply_reduce_fusion = (f32[16,2048]{1,0:T(8,128)S(1)}, f32[16,2048]{1,0:T(8,128)S(1)}, f32[16,2048]{1,0:T(8,128)S(1)}, f32[16,2048]{1,0:T(8,128)S(1)}) fusion(f32[18,34,2050]{2,0,1:T(8,128)S(1)} %fusion.1), kind=kOutput, calls=%fused_computation.6 | output fusion | flops 86900736 | bytes 34078720 | tf_op jit(solution)/shard_map/jit(cumsum)/reduce_window_sum | solution.py:41
  43.7 3.3 %collective-permute-start.4 = (f32[4,2,1,4,2048]{4,3,2,1,0:T(4,128)S(1)}, f32[4,2,1,4,2048]{4,3,2,1,0:T(4,128)S(1)}, u32[]{:S(2)}, u32[]{:S(2)}) collective-permute-start(f32[4,2,1,4,2048]{4,3,2,1,0:T(4,128)S(1)} %constant_dynamic-slice_fusion), channel_id=1, source_target_pairs={{0,1},{1,0},{2,3},{3,2},{4,5},{5,4},{6,7},{7,6},{8,9},{9,8},{10,11... | collective-permute-start | bytes 786440 | tf_op jit(solution)/shard_map/ppermute | solution.py:26
  47.0 1.2 %collective-permute-done.4 = f32[4,2,1,4,2048]{4,3,2,1,0:T(4,128)S(1)} collective-permute-done((f32[4,2,1,4,2048]{4,3,2,1,0:T(4,128)S(1)}, f32[4,2,1,4,2048]{4,3,2,1,0:T(4,128)S(1)}, u32[]{:S(2)}, u32[]{:S(2)}) %collective-permute-start.4) | collective-permute-done | bytes 262176 | tf_op jit(solution)/shard_map/ppermute | solution.py:26
  48.2 0.1 dynamic-slice_select_fusion.1
  48.3 0.1 fusion.7
  48.4 0.2 collective-permute-start.5
  48.7 5.6 %collective-permute-done.5 = f32[4,1,1,4,2048]{4,3,2,1,0:T(4,128)S(1)} collective-permute-done((f32[4,1,1,4,2048]{4,3,2,1,0:T(4,128)S(1)}, f32[4,1,1,4,2048]{4,3,2,1,0:T(4,128)S(1)}, u32[]{:S(2)}, u32[]{:S(2)}) %collective-permute-start.5) | collective-permute-done | bytes 131104 | tf_op jit(solution)/shard_map/ppermute | solution.py:26
  54.3 0.1 broadcast_select_fusion.1
  54.4 0.7 %pad_maximum_fusion = f32[4,4,2048]{2,1,0:T(4,128)} fusion(f32[1,4,2048]{2,1,0:T(4,128)S(1)} %get-tuple-element.20, f32[3,4,2048]{2,1,0:T(4,128)S(1)} %fusion.11), kind=kLoop, calls=%fused_computation.29 | loop fusion | flops 32768 | bytes 262144 | tf_op jit(solution)/shard_map/concatenate | solution.py:73
  (14 shorter events, 0.4 us)
Async XLA Ops:
  3.2 15.6 %collective-permute-start = (bf16[1,32,2048]{2,0,1:T(2,128)(2,1)S(1)}, bf16[1,32,2048]{2,0,1:T(2,128)(2,1)S(1)}, u32[]{:S(2)}, u32[]{:S(2)}) collective-permute-start(bf16[1,32,2048]{2,0,1:T(2,128)(2,1)S(1)} %get-tuple-element.11), channel_id=1, source_target_pairs={{0,4},{4,8},{8,12},{12,16},{16,20},{20,24},{24,28},{1,5},{5,9},{9,... | collective-permute-start | bytes 393224 | tf_op jit(solution)/shard_map/ppermute | solution.py:17
  6.6 12.1 %collective-permute-start.1 = (bf16[1,32,2048]{2,0,1:T(2,128)(2,1)S(1)}, bf16[1,32,2048]{2,0,1:T(2,128)(2,1)S(1)}, u32[]{:S(2)}, u32[]{:S(2)}) collective-permute-start(bf16[1,32,2048]{2,0,1:T(2,128)(2,1)S(1)} %get-tuple-element.12), channel_id=1, source_target_pairs={{4,0},{8,4},{12,8},{16,12},{20,16},{24,20},{28,24},{5,1},{9,5},{13... | collective-permute-start | bytes 393224 | tf_op jit(solution)/shard_map/ppermute | solution.py:20
  18.8 2.6 %collective-permute-start.2 = (bf16[18,1,2048]{2,0,1:T(8,128)(2,1)S(1)}, bf16[18,1,2048]{2,0,1:T(8,128)(2,1)S(1)}, u32[]{:S(2)}, u32[]{:S(2)}) collective-permute-start(bf16[18,1,2048]{2,0,1:T(8,128)(2,1)S(1)} %get-tuple-element.9), channel_id=1, source_target_pairs={{0,1},{1,2},{2,3},{4,5},{5,6},{6,7},{8,9},{9,10},{10,11},{12,13},{... | collective-permute-start | bytes 221192 | tf_op jit(solution)/shard_map/ppermute | solution.py:17
  20.1 4.9 %collective-permute-start.3 = (bf16[18,1,2048]{2,0,1:T(8,128)(2,1)S(1)}, bf16[18,1,2048]{2,0,1:T(8,128)(2,1)S(1)}, u32[]{:S(2)}, u32[]{:S(2)}) collective-permute-start(bf16[18,1,2048]{2,0,1:T(8,128)(2,1)S(1)} %get-tuple-element.10), channel_id=1, source_target_pairs={{1,0},{2,1},{3,2},{5,4},{6,5},{7,6},{9,8},{10,9},{11,10},{13,12},{... | collective-permute-start | bytes 221192 | tf_op jit(solution)/shard_map/ppermute | solution.py:20
  43.7 4.5 %collective-permute-start.4 = (f32[4,2,1,4,2048]{4,3,2,1,0:T(4,128)S(1)}, f32[4,2,1,4,2048]{4,3,2,1,0:T(4,128)S(1)}, u32[]{:S(2)}, u32[]{:S(2)}) collective-permute-start(f32[4,2,1,4,2048]{4,3,2,1,0:T(4,128)S(1)} %constant_dynamic-slice_fusion), channel_id=1, source_target_pairs={{0,1},{1,0},{2,3},{3,2},{4,5},{5,4},{6,7},{7,6},{8,9},{9,8},{10,11... | collective-permute-start | bytes 786440 | tf_op jit(solution)/shard_map/ppermute | solution.py:26
  48.4 5.8 %collective-permute-start.5 = (f32[4,1,1,4,2048]{4,3,2,1,0:T(4,128)S(1)}, f32[4,1,1,4,2048]{4,3,2,1,0:T(4,128)S(1)}, u32[]{:S(2)}, u32[]{:S(2)}) collective-permute-start(f32[4,1,1,4,2048]{4,3,2,1,0:T(4,128)S(1)} %fusion.8), channel_id=1, source_target_pairs={{0,2},{1,3},{2,0},{3,1},{4,6},{5,7},{6,4},{7,5},{8,10},{9,11},{10,... | collective-permute-start | bytes 393224 | tf_op jit(solution)/shard_map/ppermute | solution.py:26
where the time goes:
time: 56.2 us; the launch traced here: 55.1 us
  waiting for transfers between devices  20 us (36%)
  other arithmetic  19.4 us (35%)
  starting transfers between devices  12 us (21%)
  local copies, waits for them, and re-layouts  3.42 us (6%)
    another operation x1, other arithmetic, brick_image(): before = jnp.cumsum(extinct, axis=1) - extinct  12.8 us
    ppermute x2, waiting for transfers between devices, padded_2(): lax.ppermute(lax.slice_in_dim(block, block.shape[dim] - width, None, axis...  9.69 us
    ppermute x2, waiting for transfers between devices, partner_2(): lax.ppermute(x, axis, [(i, i ^ 1 << stride) for i in range(lax.axis_size(...  6.76 us
    convert_element_type x1, other arithmetic, brick_image(): field = padded.astype(jnp.float32)  5.44 us
    ppermute x2, starting transfers between devices, padded_2(): lax.ppermute(lax.slice_in_dim(block, block.shape[dim] - width, None, axis...  4.72 us
    ppermute x2, starting transfers between devices, padded_2(): lax.ppermute(lax.slice_in_dim(block, 0, width, axis=dim), axis, backward)  3.72 us
    ppermute x2, waiting for transfers between devices, padded_2(): lax.ppermute(lax.slice_in_dim(block, 0, width, axis=dim), axis, backward)  3.59 us
    ppermute x2, starting transfers between devices, partner_2(): lax.ppermute(x, axis, [(i, i ^ 1 << stride) for i in range(lax.axis_size(...  3.54 us
  transfers between devices with their start and end apart: 6, of which 4 were waited for; matrix products, arithmetic and copies ran while one was open for 0% of the time, Pallas kernels for 0%

commit v1 on v0

v1 whole, which is shorter than its diff:
```python
import math

import jax
import jax.numpy as jnp
from jax import lax
from jax.experimental import pallas as pl
from jax.experimental.pallas import tpu as pltpu
from jax.sharding import PartitionSpec as P

OPACITY = 3.0
LIGHT_X = 0.48
LIGHT_Y = 0.6
LIGHT_Z = 0.64
AMBIENT = 0.3
DIFFUSE = 0.7
LOG2E = math.log2(math.e)
LANES = 128
SUB = 8

VMEM = pl.BlockSpec(memory_space=pltpu.VMEM)
HBM = pl.BlockSpec(memory_space=pltpu.HBM)


def parity(axis):
    return lax.rem(lax.axis_index(axis), 2)


def pairs(axis, odd):
    found = []
    for low in range(odd, lax.axis_size(axis) - 1, 2):
        found += [(low, low + 1), (low + 1, low)]
    return found


def faces_kernel(volume, tile_a, tile_b, depth_a, depth_b, near, far, wide, sems):
    cells_x, cells_z, rows_y = volume.shape
    chunks = rows_y // LANES
    odd_tile = parity("tile")
    odd_depth = parity("depth")
    copies = [
        pltpu.make_async_copy(volume.at[:, pl.ds(0, SUB)], near, sems.at[0]),
        pltpu.make_async_copy(volume.at[:, pl.ds(cells_z - SUB, SUB)], far, sems.at[1]),
        pltpu.make_async_copy(volume.at[(cells_x - 1) * odd_tile], tile_b, sems.at[2]),
        pltpu.make_async_copy(volume.at[(cells_x - 1) * (1 - odd_tile)], tile_a, sems.at[3]),
    ]
    for copy in copies:
        copy.start()
    pitch = SUB + 1
    for which, (block, row) in enumerate(((near, 0), (far, SUB - 1))):
        copies[which].wait()
        for x in range(cells_x):
            rows = block[x].astype(jnp.float32)
            for c in range(chunks):
                wide[which, c, pl.ds(x * pitch, SUB), :] = rows[:, c * LANES : (c + 1) * LANES]
    for c in range(chunks):
        lanes = pl.ds(c * LANES, LANES)
        first, last = [
            jnp.concatenate(
                [
                    wide[which, c, pl.ds(g * SUB * pitch + row, SUB, stride=pitch), :]
                    for g in range(cells_x // SUB)
                ],
                axis=0,
            )
            for which, row in ((0, 0), (1, SUB - 1))
        ]
        depth_a[:, lanes] = jnp.where(odd_depth == 0, last, first).astype(jnp.bfloat16)
        depth_b[:, lanes] = jnp.where(odd_depth == 0, first, last).astype(jnp.bfloat16)
    copies[2].wait()
    copies[3].wait()


def faces(volume):
    cells_x, cells_z, rows_y = volume.shape
    column = jax.ShapeDtypeStruct((cells_z, rows_y), volume.dtype)
    layer = jax.ShapeDtypeStruct((cells_x, rows_y), volume.dtype)
    return pl.pallas_call(
        faces_kernel,
        out_shape=(column, column, layer, layer),
        in_specs=[HBM],
        out_specs=(VMEM,) * 4,
        scratch_shapes=[
            pltpu.VMEM((cells_x, SUB, rows_y), volume.dtype),
            pltpu.VMEM((cells_x, SUB, rows_y), volume.dtype),
            pltpu.VMEM((2, rows_y // LANES, cells_x * (SUB + 1), LANES), jnp.float32),
            pltpu.SemaphoreType.DMA((4,)),
        ],
        name="faces",
    )(volume)


class Field:
    def __init__(self, ref, cells_z, rows_y, slots):
        self.ref = ref
        self.cells_z = cells_z
        self.chunks = rows_y // LANES
        self.half = self.chunks // 2
        self.column, self.pitch, _ = Field.shape(cells_z, rows_y, slots)

    @staticmethod
    def shape(cells_z, rows_y, slots):
        column = cells_z + 2
        column += column % SUB == 0
        pitch = slots * column
        pitch += pitch % 4 == 0
        return column, pitch, (rows_y // LANES + 2) * pitch

    def row(self, chunk, slot, z):
        return (chunk + 1) * self.pitch + slot * self.column + z + 1

    def clear_ends(self):
        blank = jnp.zeros((self.pitch, LANES), jnp.float32)
        self.ref[pl.ds(0, self.pitch), :] = blank
        self.ref[pl.ds((self.chunks + 1) * self.pitch, self.pitch), :] = blank

    def put_column(self, slot, block):
        wide = block.astype(jnp.float32)
        for c in range(self.chunks):
            lanes = slice(c * LANES, (c + 1) * LANES)
            self.ref[pl.ds(self.row(c, slot, 0), self.cells_z), :] = wide[:, lanes]

    def put_layer(self, slot, z, layer):
        count = layer.shape[0]
        for c in range(self.chunks):
            lanes = slice(c * LANES, (c + 1) * LANES)
            at = pl.ds(self.row(c, slot, z), count, stride=self.column) if count > 1 else pl.ds(self.row(c, slot, z), 1)
            self.ref[at, :] = layer[:, lanes]

    def get(self, chunk, slot, z):
        return self.ref[pl.ds(self.row(chunk, slot, z), self.half, stride=2 * self.pitch), :]


def march(field, slot, depth_total):
    shape = (field.half, LANES)
    lane = lax.broadcasted_iota(jnp.int32, shape, 1)
    first, last = lane == 0, lane == LANES - 1
    coefficients = [2.0 * DIFFUSE * 0.5 * light for light in (LIGHT_X, LIGHT_Y, LIGHT_Z)]
    density = OPACITY / depth_total

    def cell(here, before, after, left, right, dy, sums):
        passing, total, skew, bell = sums
        dx = right - left
        dz = after - before
        facing = coefficients[0] * dx + coefficients[1] * dy + coefficients[2] * dz
        shade = AMBIENT + jnp.abs(facing) * lax.rsqrt(4.0 + dx * dx + dy * dy + dz * dz)
        squared = here * here
        power = squared * (-LOG2E)
        behind = passing * jnp.exp2(power * (density / (1.0 + squared)))
        weight = (passing - behind) * shade
        return behind, total + weight, skew + weight * jnp.tanh(here), bell + weight * jnp.exp2(power)

    one, zero = jnp.ones(shape, jnp.float32), jnp.zeros(shape, jnp.float32)
    even_sums = odd_sums = (one, zero, zero, zero)
    even_before, odd_before = field.get(0, slot, -1), field.get(1, slot, -1)
    even, odd = field.get(0, slot, 0), field.get(1, slot, 0)
    for z in range(field.cells_z):
        even_after, odd_after = field.get(0, slot, z + 1), field.get(1, slot, z + 1)
        next_even, last_odd = field.get(2, slot, z), field.get(-1, slot, z)
        up = [pltpu.roll(v, LANES - 1, 1) for v in (even, odd, next_even)]
        down = [pltpu.roll(v, 1, 1) for v in (last_odd, even, odd)]
        even_dy = jnp.where(last, up[1], up[0]) - jnp.where(first, down[0], down[1])
        odd_dy = jnp.where(last, up[2], up[1]) - jnp.where(first, down[1], down[2])
        even_sums = cell(
            even, even_before, even_after, field.get(0, slot - 1, z), field.get(0, slot + 1, z), even_dy, even_sums
        )
        odd_sums = cell(
            odd, odd_before, odd_after, field.get(1, slot - 1, z), field.get(1, slot + 1, z), odd_dy, odd_sums
        )
        even_before, even, odd_before, odd = even, even_after, odd, odd_after
    return [
        (0.5 * (total + skew), 0.5 * bell, 0.5 * (total - skew), passing)
        for passing, total, skew, bell in (even_sums, odd_sums)
    ]


def store_column(out, x, parts):
    for which, channels in enumerate(parts):
        for channel, value in enumerate(channels):
            out[x, channel, pl.ds(which, value.shape[0], stride=2), :] = value


def inner_kernel(depth_total, volume, depth_a, depth_b, out, scratch):
    cells_x, cells_z, rows_y = volume.shape
    field = Field(scratch, cells_z, rows_y, cells_x)
    odd_depth = parity("depth")
    field.clear_ends()
    layers = [depth_a[...].astype(jnp.float32), depth_b[...].astype(jnp.float32)]
    for layer, other in zip(layers, (odd_depth, 1 - odd_depth)):
        z = cells_z - other * (cells_z + 1)
        for x in range(0, cells_x, SUB):
            field.put_layer(x, z, layer[x : x + SUB])
    field.put_column(0, volume[0])
    field.put_column(1, volume[1])

    def column(x, _):
        field.put_column(x + 1, volume[x + 1])
        store_column(out, x - 1, march(field, x, depth_total))
        return 0

    lax.fori_loop(1, cells_x - 1, column, 0)


def inner(volume, depth_a, depth_b, depth_total):
    cells_x, cells_z, rows_y = volume.shape
    _, _, rows = Field.shape(cells_z, rows_y, cells_x)
    return pl.pallas_call(
        lambda *refs: inner_kernel(depth_total, *refs),
        out_shape=jax.ShapeDtypeStruct((cells_x - 2, 4, rows_y // LANES, LANES), jnp.float32),
        in_specs=[VMEM] * 3,
        out_specs=VMEM,
        scratch_shapes=[pltpu.VMEM((rows, LANES), jnp.float32)],
        compiler_params=pltpu.CompilerParams(vmem_limit_bytes=24 << 20),
        cost_estimate=pl.CostEstimate(flops=10**8, bytes_accessed=10**7, transcendentals=0),
        name="inner",
    )(volume, depth_a, depth_b)


def outer_kernel(depth_total, volume, depth_a, depth_b, tile_a, tile_b, done, kept, given, scratch, edge):
    cells_x, cells_z, rows_y = volume.shape
    field = Field(scratch, cells_z, rows_y, 6)
    odd_depth, odd_tile = parity("depth"), parity("tile")
    field.clear_ends()
    for slot, x in ((1, 0), (2, 1), (3, cells_x - 2), (4, cells_x - 1)):
        field.put_column(slot, volume[x])
    for block, other in ((tile_a, odd_tile), (tile_b, 1 - odd_tile)):
        field.put_column(5 * (1 - other), block[...])
    for block, other in ((depth_a, odd_depth), (depth_b, 1 - odd_depth)):
        z = cells_z - other * (cells_z + 1)
        layer = block[...].astype(jnp.float32)
        field.put_layer(1, z, layer[:1])
        field.put_layer(4, z, layer[cells_x - 1 :])

    def column(side, _):
        store_column(edge, side, march(field, 1 + 3 * side, depth_total))
        return 0

    lax.fori_loop(0, 2, column, 0)
    upper = parity("depth")
    pieces = cells_x // lax.axis_size("depth")

    def fetch(x):
        return jnp.where(x == 0, edge[0], jnp.where(x == cells_x - 1, edge[1], done[jnp.clip(x - 1, 0, cells_x - 3)]))

    for i in range(cells_x // 2):
        low = i // pieces * 2 * pieces + i % pieces
        kept[i] = fetch(low + upper * pieces)
        given[i] = fetch(low + (1 - upper) * pieces)


def outer(volume, depth_a, depth_b, tile_a, tile_b, done, depth_total):
    cells_x, cells_z, rows_y = volume.shape
    _, _, rows = Field.shape(cells_z, rows_y, 6)
    half = jax.ShapeDtypeStruct((cells_x // 2, 4, rows_y // LANES, LANES), jnp.float32)
    return pl.pallas_call(
        lambda *refs: outer_kernel(depth_total, *refs),
        out_shape=(half, half),
        in_specs=[VMEM] * 6,
        out_specs=(VMEM, VMEM),
        scratch_shapes=[
            pltpu.VMEM((rows, LANES), jnp.float32),
            pltpu.VMEM((2, 4, rows_y // LANES, LANES), jnp.float32),
        ],
        compiler_params=pltpu.CompilerParams(vmem_limit_bytes=24 << 20),
        cost_estimate=pl.CostEstimate(flops=10**7, bytes_accessed=10**6, transcendentals=0),
        name="outer",
    )(volume, depth_a, depth_b, tile_a, tile_b, done)


def over(own, other, in_front):
    front = [jnp.where(in_front, a, b) for a, b in zip(own, other)]
    back = [jnp.where(in_front, b, a) for a, b in zip(own, other)]
    return [a + front[3] * b for a, b in zip(front[:3], back[:3])] + [front[3] * back[3]]


def merge_kernel(section, pieces, kept, other, next_kept, next_given):
    position = lax.axis_index("depth")
    in_front = lax.rem(position // 2**section, 2) == 0
    upper = lax.rem(position // 2 ** (section + 1), 2)
    for i in range(kept.shape[0] // 2):
        low = i // pieces * 2 * pieces + i % pieces
        for target, x in ((next_kept, low + upper * pieces), (next_given, low + (1 - upper) * pieces)):
            for channel, value in enumerate(over(list(kept[x]), list(other[x]), in_front)):
                target[i, channel] = value


def merge(kept, other, section, pieces):
    half = jax.ShapeDtypeStruct((kept.shape[0] // 2, *kept.shape[1:]), kept.dtype)
    return pl.pallas_call(
        lambda *refs: merge_kernel(section, pieces, *refs),
        out_shape=(half, half),
        in_specs=[VMEM] * 2,
        out_specs=(VMEM, VMEM),
        name="merge",
    )(kept, other)


def finish_kernel(section, kept, other, image, whole):
    position = lax.axis_index("depth")
    in_front = lax.rem(position // 2**section, 2) == 0
    columns, _, chunks, _ = kept.shape
    for x in range(columns):
        red, green, blue, passing = over(list(kept[x]), list(other[x]), in_front)
        for channel, value in enumerate((red, green, blue, 1.0 - passing)):
            for c in range(chunks):
                image[channel, pl.ds(x, 1), pl.ds(c * LANES, LANES)] = value[c : c + 1]


def finish(kept, other, section):
    columns, channels, chunks, _ = kept.shape
    return pl.pallas_call(
        lambda section_kept, section_other, image: finish_kernel(section, section_kept, section_other, image, None),
        out_shape=jax.ShapeDtypeStruct((channels, columns, chunks * LANES), kept.dtype),
        in_specs=[VMEM] * 2,
        out_specs=VMEM,
        name="finish",
    )(kept, other)


def shards(volume):
    depth_count = lax.axis_size("depth")
    depth_total = volume.shape[1] * depth_count
    pieces = volume.shape[0] // depth_count
    levels = depth_count.bit_length() - 1
    tile_a, tile_b, depth_a, depth_b = faces(volume)
    tile_b = lax.ppermute(tile_b, "tile", pairs("tile", 1))
    depth_b = lax.ppermute(depth_b, "depth", pairs("depth", 1))
    depth_a = lax.ppermute(depth_a, "depth", pairs("depth", 0))
    tile_a = lax.ppermute(tile_a, "tile", pairs("tile", 0))
    done = inner(volume, depth_a, depth_b, depth_total)
    kept, given = outer(volume, depth_a, depth_b, tile_a, tile_b, done, depth_total)
    for section in range(levels):
        other = lax.ppermute(given, "depth", [(i, i ^ 1 << section) for i in range(depth_count)])
        if section < levels - 1:
            kept, given = merge(kept, other, section, pieces)
    return finish(kept, other, levels - 1)


def solution(mesh):
    in_specs = (P("tile", "depth", None),)
    out_specs = P(None, ("tile", "depth"), None)
    return jax.shard_map(shards, mesh=mesh, in_specs=in_specs, out_specs=out_specs, check_vma=False)
```

time: 56.2 us -> 32.9 us (0.59); the launches traced: 55.1 us -> 32.7 us
  other arithmetic: 19.4 us -> 0 us
  waiting for transfers between devices: 20 us -> 6.56 us
  Pallas kernels: 0 us -> 12.1 us
  local copies, waits for them, and re-layouts: 3.42 us -> 2.06 us
    ppermute x6, waiting for transfers between devices: 20 us -> 6.56 us  [the longest x2 5.77 us: shards(): lax.ppermute(given, 'depth', [(i, i ^ 1 << section) for i in range(depth_...]
    another operation x1 -> x0, other arithmetic: 12.8 us -> none  [brick_image(): before = jnp.cumsum(extinct, axis=1) - extinct]
    pallas_call x0 -> x5, Pallas kernels: none -> 12.1 us  [the longest x1 5.53 us: inner(): pl.pallas_call(lambda *refs: inner_kernel(depth_total, *refs), out_shape=...]
    convert_element_type x1 -> x0, other arithmetic: 5.44 us -> none  [brick_image(): field = padded.astype(jnp.float32)]
    unnamed x4 -> x8, local copies, waits for them, and re-layouts: 2.79 us -> 2.06 us
    concatenate x2 -> x0, other arithmetic: 0.73 us -> none  [the longest x1 0.69 us: shards(): return jnp.concatenate([colour, 1.0 - passing], 0)]
  transfers between devices with their start and end apart: 6 -> 6, of which waited for: 4 -> 3; matrix products, arithmetic and copies ran while one was open for 0% -> 0% of each run, Pallas kernels for 0% -> 17%
where the time goes in v1:
time: 32.9 us; the launch traced here: 32.7 us
  Pallas kernels  12.1 us (37%)
  starting transfers between devices  11.9 us (36%)
  waiting for transfers between devices  6.56 us (20%)
  local copies, waits for them, and re-layouts  2.06 us (6%)
    ppermute x2, starting transfers between devices, shards(): lax.ppermute(given, 'depth', [(i, i ^ 1 << section) for i in range(depth_...  6.2 us
    ppermute x2, waiting for transfers between devices, shards(): lax.ppermute(given, 'depth', [(i, i ^ 1 << section) for i in range(depth_...  5.77 us
    pallas_call x1, Pallas kernels, inner(): pl.pallas_call(lambda *refs: inner_kernel(depth_total, *refs), out_shape=...  5.53 us
    ppermute x1, starting transfers between devices, shards(): tile_b = lax.ppermute(tile_b, 'tile', pairs('tile', 1))  4.92 us
    pallas_call x1, Pallas kernels, faces(): pl.pallas_call(faces_kernel, out_shape=(column, column, layer, layer), in...  2.21 us
    unnamed x8, local copies, waits for them, and re-layouts  2.06 us
    pallas_call x1, Pallas kernels, merge(): pl.pallas_call(lambda *refs: merge_kernel(section, pieces, *refs), out_sh...  1.76 us
    pallas_call x1, Pallas kernels, finish(): pl.pallas_call(lambda section_kept, section_other, image: finish_kernel(s...  1.7 us
  transfers between devices with their start and end apart: 6, of which 3 were waited for; matrix products, arithmetic and copies ran while one was open for 0% of the time, Pallas kernels for 17%

profile of v1, /device:TPU:4, one launch (start us, length us, event | category | flops | bytes accessed | tf_op | source)
XLA Modules:
  0.0 32.7 jit_solution(6629019470969414746)
XLA Ops:
  0.0 0.0 copy-start
  0.0 2.2 %faces.1 = (bf16[32,2048]{1,0:T(8,128)(2,1)}, bf16[32,2048]{1,0:T(8,128)(2,1)}, bf16[16,2048]{1,0:T(8,128)(2,1)}, bf16[16,2048]{1,0:T(8,128)(2,1)}) custom-call(bf16[16,32,2048]{2,1,0:T(8,128)(2,1)} %refs_0_.3), custom_call_target="tpu_custom_call" | custom-call | tf_op jit(solution)/shard_map/faces/pallas_call | solution.py:77
  2.2 0.1 collective-permute-start.2
  2.3 4.9 %collective-permute-start.3 = (bf16[32,2048]{1,0:T(8,128)(2,1)}, bf16[32,2048]{1,0:T(8,128)(2,1)S(1)}, u32[]{:S(2)}, u32[]{:S(2)}) collective-permute-start(bf16[32,2048]{1,0:T(8,128)(2,1)} %get-tuple-element.16), channel_id=1, source_target_pairs={{4,8},{8,4},{12,16},{16,12},{20,24},{24,20},{5,9},{9,5},{13,17},{1... | collective-permute-start | bytes 393224 | tf_op jit(solution)/shard_map/ppermute | solution.py:325
  7.2 0.1 collective-permute-start
  7.3 0.7 %collective-permute-start.1 = (bf16[16,2048]{1,0:T(8,128)(2,1)}, bf16[16,2048]{1,0:T(8,128)(2,1)S(1)}, u32[]{:S(2)}, u32[]{:S(2)}) collective-permute-start(bf16[16,2048]{1,0:T(8,128)(2,1)} %get-tuple-element.14), channel_id=1, source_target_pairs={{1,2},{2,1},{5,6},{6,5},{9,10},{10,9},{13,14},{14,13},{17,18},{18,... | collective-permute-start | bytes 196616 | tf_op jit(solution)/shard_map/ppermute | solution.py:326
  8.0 0.8 %collective-permute-done.refs_1_ = bf16[16,2048]{1,0:T(8,128)(2,1)S(1)} collective-permute-done((bf16[16,2048]{1,0:T(8,128)(2,1)}, bf16[16,2048]{1,0:T(8,128)(2,1)S(1)}, u32[]{:S(2)}, u32[]{:S(2)}) %collective-permute-start) | collective-permute-done | bytes 65568 | tf_op jit(solution)/shard_map/ppermute | solution.py:327
  8.8 0.0 collective-permute-done.1.refs_2_
  8.8 0.0 copy-done
  8.8 5.5 %inner.1.refs_5_ = f32[14,4,16,128]{3,2,1,0:T(8,128)S(1)} custom-call(bf16[16,32,2048]{2,1,0:T(8,128)(2,1)S(1)} %copy-done, bf16[16,2048]{1,0:T(8,128)(2,1)S(1)} %collective-permute-done.refs_1_, bf16[16,2048]{1,0:T(8,128)(2,1)S(1)} %collective-permute-done.1.refs_2_), custom_call_target="tpu_custom_call" | custom-call | flops 100000000 | bytes 10000000 | tf_op jit(solution)/shard_map/inner/pallas_call | solution.py:206
  14.3 0.0 collective-permute-done.2.refs_3_
  14.3 0.0 collective-permute-done.3.refs_4_
  14.3 0.9 %outer.1 = (f32[8,4,16,128]{3,2,1,0:T(8,128)S(1)}, f32[8,4,16,128]{3,2,1,0:T(8,128)S(1)}) custom-call(bf16[16,32,2048]{2,1,0:T(8,128)(2,1)S(1)} %copy-done, bf16[16,2048]{1,0:T(8,128)(2,1)S(1)} %collective-permute-done.refs_1_, bf16[16,2048]{1,0:T(8,128)(2,1)S(1)} %collective-permute-done.1.refs_2_, bf16[32,2048]{1,0:T(8,128)(2,1)S(1)} %collective-permute-done.2.refs_3_, ...), custom_call_target="tpu_custom_call" | custom-call | flops 10000000 | bytes 1000000 | tf_op jit(solution)/shard_map/outer/pallas_call | solution.py:254
  15.2 0.0 copy-start.1
  15.3 0.7 %copy-done.1 = f32[8,4,16,128]{3,2,1,0:T(8,128)} copy-done((f32[8,4,16,128]{3,2,1,0:T(8,128)}, f32[8,4,16,128]{3,2,1,0:T(8,128)S(1)}, u32[]{:S(2)}) %copy-start.1) | copy-done | bytes 262168
  15.9 4.8 %collective-permute-start.4 = (f32[8,4,16,128]{3,2,1,0:T(8,128)S(1)}, f32[8,4,16,128]{3,2,1,0:T(8,128)S(1)}, u32[]{:S(2)}, u32[]{:S(2)}) collective-permute-start(f32[8,4,16,128]{3,2,1,0:T(8,128)S(1)} %get-tuple-element.18), channel_id=1, source_target_pairs={{0,1},{1,0},{2,3},{3,2},{4,5},{5,4},{6,7},{7,6},{8,9},{9,8},{10,11... | collective-permute-start | bytes 786440 | tf_op jit(solution)/shard_map/ppermute | solution.py:332
  20.8 1.2 %collective-permute-done.4.refs_1_ = f32[8,4,16,128]{3,2,1,0:T(8,128)S(1)} collective-permute-done((f32[8,4,16,128]{3,2,1,0:T(8,128)S(1)}, f32[8,4,16,128]{3,2,1,0:T(8,128)S(1)}, u32[]{:S(2)}, u32[]{:S(2)}) %collective-permute-start.4) | collective-permute-done | bytes 262176 | tf_op jit(solution)/shard_map/ppermute | solution.py:332
  21.9 0.0 copy-start.2
  21.9 0.7 %copy-done.2 = f32[8,4,16,128]{3,2,1,0:T(8,128)} copy-done((f32[8,4,16,128]{3,2,1,0:T(8,128)}, f32[8,4,16,128]{3,2,1,0:T(8,128)S(1)}, u32[]{:S(2)}) %copy-start.2) | copy-done | bytes 262168
  22.6 1.8 %merge.1 = (f32[4,4,16,128]{3,2,1,0:T(8,128)}, f32[4,4,16,128]{3,2,1,0:T(8,128)}) custom-call(f32[8,4,16,128]{3,2,1,0:T(8,128)} %copy-done.1, f32[8,4,16,128]{3,2,1,0:T(8,128)} %copy-done.2), custom_call_target="tpu_custom_call" | custom-call | tf_op jit(solution)/shard_map/merge/pallas_call | solution.py:288
  24.4 1.4 %collective-permute-start.5 = (f32[4,4,16,128]{3,2,1,0:T(8,128)}, f32[4,4,16,128]{3,2,1,0:T(8,128)S(1)}, u32[]{:S(2)}, u32[]{:S(2)}) collective-permute-start(f32[4,4,16,128]{3,2,1,0:T(8,128)} %get-tuple-element.20), channel_id=1, source_target_pairs={{0,2},{1,3},{2,0},{3,1},{4,6},{5,7},{6,4},{7,5},{8,10},{9,11},{10,... | collective-permute-start | bytes 393224 | tf_op jit(solution)/shard_map/ppermute | solution.py:332
  25.8 4.6 %collective-permute-done.5.section_other = f32[4,4,16,128]{3,2,1,0:T(8,128)S(1)} collective-permute-done((f32[4,4,16,128]{3,2,1,0:T(8,128)}, f32[4,4,16,128]{3,2,1,0:T(8,128)S(1)}, u32[]{:S(2)}, u32[]{:S(2)}) %collective-permute-start.5) | collective-permute-done | bytes 131104 | tf_op jit(solution)/shard_map/ppermute | solution.py:332
  30.4 0.6 %copy-done.3 = f32[4,4,16,128]{3,2,1,0:T(8,128)} copy-done((f32[4,4,16,128]{3,2,1,0:T(8,128)}, f32[4,4,16,128]{3,2,1,0:T(8,128)S(1)}, u32[]{:S(2)}) %copy-start.3) | copy-done | bytes 131096
  31.0 1.7 %finish.1 = f32[4,4,2048]{2,1,0:T(4,128)} custom-call(f32[4,4,16,128]{3,2,1,0:T(8,128)} %get-tuple-element.19.section_kept, f32[4,4,16,128]{3,2,1,0:T(8,128)} %copy-done.3), custom_call_target="tpu_custom_call" | custom-call | tf_op jit(solution)/shard_map/finish/pallas_call | solution.py:310
  (1 shorter events, 0.0 us)
Async XLA Ops:
  0.0 8.8 %copy-start = (bf16[16,32,2048]{2,1,0:T(8,128)(2,1)S(1)}, bf16[16,32,2048]{2,1,0:T(8,128)(2,1)}, u32[]{:S(2)}) copy-start(bf16[16,32,2048]{2,1,0:T(8,128)(2,1)} %refs_0_.3) | copy-start | bytes 6291460
  2.2 12.1 %collective-permute-start.2 = (bf16[32,2048]{1,0:T(8,128)(2,1)}, bf16[32,2048]{1,0:T(8,128)(2,1)S(1)}, u32[]{:S(2)}, u32[]{:S(2)}) collective-permute-start(bf16[32,2048]{1,0:T(8,128)(2,1)} %get-tuple-element.15), channel_id=1, source_target_pairs={{0,4},{4,0},{8,12},{12,8},{16,20},{20,16},{24,28},{28,24},{1,5},{5... | collective-permute-start | bytes 393224 | tf_op jit(solution)/shard_map/ppermute | solution.py:328
  2.3 12.0 %collective-permute-start.3 = (bf16[32,2048]{1,0:T(8,128)(2,1)}, bf16[32,2048]{1,0:T(8,128)(2,1)S(1)}, u32[]{:S(2)}, u32[]{:S(2)}) collective-permute-start(bf16[32,2048]{1,0:T(8,128)(2,1)} %get-tuple-element.16), channel_id=1, source_target_pairs={{4,8},{8,4},{12,16},{16,12},{20,24},{24,20},{5,9},{9,5},{13,17},{1... | collective-permute-start | bytes 393224 | tf_op jit(solution)/shard_map/ppermute | solution.py:325
  7.2 1.5 %collective-permute-start = (bf16[16,2048]{1,0:T(8,128)(2,1)}, bf16[16,2048]{1,0:T(8,128)(2,1)S(1)}, u32[]{:S(2)}, u32[]{:S(2)}) collective-permute-start(bf16[16,2048]{1,0:T(8,128)(2,1)} %get-tuple-element.13), channel_id=1, source_target_pairs={{0,1},{1,0},{2,3},{3,2},{4,5},{5,4},{6,7},{7,6},{8,9},{9,8},{10,11... | collective-permute-start | bytes 196616 | tf_op jit(solution)/shard_map/ppermute | solution.py:327
  7.3 1.5 %collective-permute-start.1 = (bf16[16,2048]{1,0:T(8,128)(2,1)}, bf16[16,2048]{1,0:T(8,128)(2,1)S(1)}, u32[]{:S(2)}, u32[]{:S(2)}) collective-permute-start(bf16[16,2048]{1,0:T(8,128)(2,1)} %get-tuple-element.14), channel_id=1, source_target_pairs={{1,2},{2,1},{5,6},{6,5},{9,10},{10,9},{13,14},{14,13},{17,18},{18,... | collective-permute-start | bytes 196616 | tf_op jit(solution)/shard_map/ppermute | solution.py:326
  15.2 0.7 %copy-start.1 = (f32[8,4,16,128]{3,2,1,0:T(8,128)}, f32[8,4,16,128]{3,2,1,0:T(8,128)S(1)}, u32[]{:S(2)}) copy-start(f32[8,4,16,128]{3,2,1,0:T(8,128)S(1)} %get-tuple-element.17.refs_0_) | copy-start | bytes 786436
  15.9 6.0 %collective-permute-start.4 = (f32[8,4,16,128]{3,2,1,0:T(8,128)S(1)}, f32[8,4,16,128]{3,2,1,0:T(8,128)S(1)}, u32[]{:S(2)}, u32[]{:S(2)}) collective-permute-start(f32[8,4,16,128]{3,2,1,0:T(8,128)S(1)} %get-tuple-element.18), channel_id=1, source_target_pairs={{0,1},{1,0},{2,3},{3,2},{4,5},{5,4},{6,7},{7,6},{8,9},{9,8},{10,11... | collective-permute-start | bytes 786440 | tf_op jit(solution)/shard_map/ppermute | solution.py:332
  21.9 0.7 %copy-start.2 = (f32[8,4,16,128]{3,2,1,0:T(8,128)}, f32[8,4,16,128]{3,2,1,0:T(8,128)S(1)}, u32[]{:S(2)}) copy-start(f32[8,4,16,128]{3,2,1,0:T(8,128)S(1)} %collective-permute-done.4.refs_1_) | copy-start | bytes 786436
  24.4 6.0 %collective-permute-start.5 = (f32[4,4,16,128]{3,2,1,0:T(8,128)}, f32[4,4,16,128]{3,2,1,0:T(8,128)S(1)}, u32[]{:S(2)}, u32[]{:S(2)}) collective-permute-start(f32[4,4,16,128]{3,2,1,0:T(8,128)} %get-tuple-element.20), channel_id=1, source_target_pairs={{0,2},{1,3},{2,0},{3,1},{4,6},{5,7},{6,4},{7,5},{8,10},{9,11},{10,... | collective-permute-start | bytes 393224 | tf_op jit(solution)/shard_map/ppermute | solution.py:332
  30.4 0.7 %copy-start.3 = (f32[4,4,16,128]{3,2,1,0:T(8,128)}, f32[4,4,16,128]{3,2,1,0:T(8,128)S(1)}, u32[]{:S(2)}) copy-start(f32[4,4,16,128]{3,2,1,0:T(8,128)S(1)} %collective-permute-done.5.section_other) | copy-start | bytes 393220

commit v2 on v1

--- a/solution.py
+++ b/solution.py
@@ -6,6 +6,7 @@
 from jax.experimental import pallas as pl
 from jax.experimental.pallas import tpu as pltpu
 from jax.sharding import PartitionSpec as P
+
 
 OPACITY = 3.0
 LIGHT_X = 0.48
@@ -85,8 +86,9 @@
             pltpu.VMEM((2, rows_y // LANES, cells_x * (SUB + 1), LANES), jnp.float32),
             pltpu.SemaphoreType.DMA((4,)),
         ],
+        compiler_params=pltpu.CompilerParams(vmem_limit_bytes=12 << 20),
         name="faces",
-    )(volume)
+    )(pltpu.with_memory_space_constraint(volume, pltpu.HBM))
 
 
 class Field:
@@ -290,11 +292,12 @@
         out_shape=(half, half),
         in_specs=[VMEM] * 2,
         out_specs=(VMEM, VMEM),
+        compiler_params=pltpu.CompilerParams(vmem_limit_bytes=8 << 20),
         name="merge",
     )(kept, other)
 
 
-def finish_kernel(section, kept, other, image, whole):
+def finish_kernel(section, kept, other, image):
     position = lax.axis_index("depth")
     in_front = lax.rem(position // 2**section, 2) == 0
     columns, _, chunks, _ = kept.shape
@@ -308,10 +311,11 @@
 def finish(kept, other, section):
     columns, channels, chunks, _ = kept.shape
     return pl.pallas_call(
-        lambda section_kept, section_other, image: finish_kernel(section, section_kept, section_other, image, None),
+        lambda section_kept, section_other, image: finish_kernel(section, section_kept, section_other, image),
         out_shape=jax.ShapeDtypeStruct((channels, columns, chunks * LANES), kept.dtype),
         in_specs=[VMEM] * 2,
         out_specs=VMEM,
+        compiler_params=pltpu.CompilerParams(vmem_limit_bytes=8 << 20),
         name="finish",
     )(kept, other)
 

time: 32.9 us -> 27.1 us (0.82)
  Pallas kernels: 12.1 us -> 8.69 us
  local copies, waits for them, and re-layouts: 2.06 us -> 0.01 us
  waiting for transfers between devices: 6.56 us -> 6.13 us
    unnamed x8 -> x2, local copies, waits for them, and re-layouts: 2.06 us -> 0.01 us
    pallas_call x1, Pallas kernels: 1.76 us -> 0.04 us  [merge(): pl.pallas_call(lambda *refs: merge_kernel(section, pieces, *refs), out_sh...]
    pallas_call x1, Pallas kernels: 1.7 us -> 0.73 us  [finish(): pl.pallas_call(lambda section_kept, section_other, image: finish_kernel(s...]
    pallas_call x1, Pallas kernels: 2.21 us -> 1.48 us  [faces(): pl.pallas_call(faces_kernel, out_shape=(column, column, layer, layer), in...]
  transfers between devices with their start and end apart: 6 -> 6, of which waited for: 3 -> 3; matrix products, arithmetic and copies ran while one was open for 0% -> 0% of each run, Pallas kernels for 17% -> 20%
where the time goes in v2:
time: 27.1 us; the launch traced here: 27 us
  starting transfers between devices  12.1 us (45%)
  Pallas kernels  8.69 us (32%)
  waiting for transfers between devices  6.13 us (23%)
    ppermute x2, starting transfers between devices, shards(): lax.ppermute(given, 'depth', [(i, i ^ 1 << section) for i in range(depth_...  6.33 us
    ppermute x2, waiting for transfers between devices, shards(): lax.ppermute(given, 'depth', [(i, i ^ 1 << section) for i in range(depth_...  5.56 us
    pallas_call x1, Pallas kernels, inner(): pl.pallas_call(lambda *refs: inner_kernel(depth_total, *refs), out_shape=...  5.53 us
    ppermute x1, starting transfers between devices, shards(): tile_b = lax.ppermute(tile_b, 'tile', pairs('tile', 1))  4.92 us
    pallas_call x1, Pallas kernels, faces(): pl.pallas_call(faces_kernel, out_shape=(column, column, layer, layer), in...  1.48 us
    pallas_call x1, Pallas kernels, outer(): pl.pallas_call(lambda *refs: outer_kernel(depth_total, *refs), out_shape=...  0.91 us
    pallas_call x1, Pallas kernels, finish(): pl.pallas_call(lambda section_kept, section_other, image: finish_kernel(s...  0.73 us
    ppermute x1, starting transfers between devices, shards(): depth_b = lax.ppermute(depth_b, 'depth', pairs('depth', 1))  0.66 us
  transfers between devices with their start and end apart: 6, of which 3 were waited for; matrix products, arithmetic and copies ran while one was open for 0% of the time, Pallas kernels for 20%

profile of v2, /device:TPU:4, one launch (start us, length us, event | category | flops | bytes accessed | tf_op | source)
XLA Modules:
  0.0 27.0 jit_solution(14236101715923147085)
XLA Ops:
  0.0 0.0 copy-start
  0.0 1.5 %faces.1 = (bf16[32,2048]{1,0:T(8,128)(2,1)S(1)}, bf16[32,2048]{1,0:T(8,128)(2,1)S(1)}, bf16[16,2048]{1,0:T(8,128)(2,1)S(1)}, bf16[16,2048]{1,0:T(8,128)(2,1)S(1)}) custom-call(bf16[16,32,2048]{2,1,0:T(8,128)(2,1)} %refs_0_.3), custom_call_target="tpu_custom_call" | custom-call | tf_op jit(solution)/shard_map/faces/pallas_call | solution.py:78
  1.5 0.1 collective-permute-start.2
  1.6 4.9 %collective-permute-start.3 = (bf16[32,2048]{1,0:T(8,128)(2,1)S(1)}, bf16[32,2048]{1,0:T(8,128)(2,1)S(1)}, u32[]{:S(2)}, u32[]{:S(2)}) collective-permute-start(bf16[32,2048]{1,0:T(8,128)(2,1)S(1)} %get-tuple-element.16), channel_id=1, source_target_pairs={{4,8},{8,4},{12,16},{16,12},{20,24},{24,20},{5,9},{9,5},{13,17},{1... | collective-permute-start | bytes 393224 | tf_op jit(solution)/shard_map/ppermute | solution.py:329
  6.5 0.1 collective-permute-start
  6.6 0.7 %collective-permute-start.1 = (bf16[16,2048]{1,0:T(8,128)(2,1)S(1)}, bf16[16,2048]{1,0:T(8,128)(2,1)S(1)}, u32[]{:S(2)}, u32[]{:S(2)}) collective-permute-start(bf16[16,2048]{1,0:T(8,128)(2,1)S(1)} %get-tuple-element.14), channel_id=1, source_target_pairs={{1,2},{2,1},{5,6},{6,5},{9,10},{10,9},{13,14},{14,13},{17,18},{18,... | collective-permute-start | bytes 196616 | tf_op jit(solution)/shard_map/ppermute | solution.py:330
  7.2 0.6 %collective-permute-done.refs_1_ = bf16[16,2048]{1,0:T(8,128)(2,1)S(1)} collective-permute-done((bf16[16,2048]{1,0:T(8,128)(2,1)S(1)}, bf16[16,2048]{1,0:T(8,128)(2,1)S(1)}, u32[]{:S(2)}, u32[]{:S(2)}) %collective-permute-start) | collective-permute-done | bytes 65568 | tf_op jit(solution)/shard_map/ppermute | solution.py:331
  7.8 0.0 collective-permute-done.1.refs_2_
  7.8 0.0 copy-done
  7.8 5.5 %inner.1.refs_5_ = f32[14,4,16,128]{3,2,1,0:T(8,128)S(1)} custom-call(bf16[16,32,2048]{2,1,0:T(8,128)(2,1)S(1)} %copy-done, bf16[16,2048]{1,0:T(8,128)(2,1)S(1)} %collective-permute-done.refs_1_, bf16[16,2048]{1,0:T(8,128)(2,1)S(1)} %collective-permute-done.1.refs_2_), custom_call_target="tpu_custom_call" | custom-call | flops 100000000 | bytes 10000000 | tf_op jit(solution)/shard_map/inner/pallas_call | solution.py:208
  13.4 0.0 collective-permute-done.2.refs_3_
  13.4 0.0 collective-permute-done.3.refs_4_
  13.4 0.9 %outer.1 = (f32[8,4,16,128]{3,2,1,0:T(8,128)S(1)}, f32[8,4,16,128]{3,2,1,0:T(8,128)S(1)}) custom-call(bf16[16,32,2048]{2,1,0:T(8,128)(2,1)S(1)} %copy-done, bf16[16,2048]{1,0:T(8,128)(2,1)S(1)} %collective-permute-done.refs_1_, bf16[16,2048]{1,0:T(8,128)(2,1)S(1)} %collective-permute-done.1.refs_2_, bf16[32,2048]{1,0:T(8,128)(2,1)S(1)} %collective-permute-done.2.refs_3_, ...), custom_call_target="tpu_custom_call" | custom-call | flops 10000000 | bytes 1000000 | tf_op jit(solution)/shard_map/outer/pallas_call | solution.py:256
  14.3 4.9 %collective-permute-start.4 = (f32[8,4,16,128]{3,2,1,0:T(8,128)S(1)}, f32[8,4,16,128]{3,2,1,0:T(8,128)S(1)}, u32[]{:S(2)}, u32[]{:S(2)}) collective-permute-start(f32[8,4,16,128]{3,2,1,0:T(8,128)S(1)} %get-tuple-element.18), channel_id=1, source_target_pairs={{0,1},{1,0},{2,3},{3,2},{4,5},{5,4},{6,7},{7,6},{8,9},{9,8},{10,11... | collective-permute-start | bytes 786440 | tf_op jit(solution)/shard_map/ppermute | solution.py:336
  19.2 1.2 %collective-permute-done.4.refs_1_ = f32[8,4,16,128]{3,2,1,0:T(8,128)S(1)} collective-permute-done((f32[8,4,16,128]{3,2,1,0:T(8,128)S(1)}, f32[8,4,16,128]{3,2,1,0:T(8,128)S(1)}, u32[]{:S(2)}, u32[]{:S(2)}) %collective-permute-start.4) | collective-permute-done | bytes 262176 | tf_op jit(solution)/shard_map/ppermute | solution.py:336
  20.4 1.4 %collective-permute-start.5 = (f32[4,4,16,128]{3,2,1,0:T(8,128)S(1)}, f32[4,4,16,128]{3,2,1,0:T(8,128)S(1)}, u32[]{:S(2)}, u32[]{:S(2)}) collective-permute-start(f32[4,4,16,128]{3,2,1,0:T(8,128)S(1)} %get-tuple-element.20), channel_id=1, source_target_pairs={{0,2},{1,3},{2,0},{3,1},{4,6},{5,7},{6,4},{7,5},{8,10},{9,11},{10,... | collective-permute-start | bytes 393224 | tf_op jit(solution)/shard_map/ppermute | solution.py:336
  21.8 4.4 %collective-permute-done.5.section_other = f32[4,4,16,128]{3,2,1,0:T(8,128)S(1)} collective-permute-done((f32[4,4,16,128]{3,2,1,0:T(8,128)S(1)}, f32[4,4,16,128]{3,2,1,0:T(8,128)S(1)}, u32[]{:S(2)}, u32[]{:S(2)}) %collective-permute-start.5) | collective-permute-done | bytes 131104 | tf_op jit(solution)/shard_map/ppermute | solution.py:336
  26.2 0.7 %finish.1 = f32[4,4,2048]{2,1,0:T(4,128)} custom-call(f32[4,4,16,128]{3,2,1,0:T(8,128)S(1)} %get-tuple-element.19.section_kept, f32[4,4,16,128]{3,2,1,0:T(8,128)S(1)} %collective-permute-done.5.section_other), custom_call_target="tpu_custom_call" | custom-call | tf_op jit(solution)/shard_map/finish/pallas_call | solution.py:313
  (1 shorter events, 0.0 us)
Async XLA Ops:
  0.0 7.8 %copy-start = (bf16[16,32,2048]{2,1,0:T(8,128)(2,1)S(1)}, bf16[16,32,2048]{2,1,0:T(8,128)(2,1)}, u32[]{:S(2)}) copy-start(bf16[16,32,2048]{2,1,0:T(8,128)(2,1)} %refs_0_.3) | copy-start | bytes 6291460
  1.5 11.9 %collective-permute-start.2 = (bf16[32,2048]{1,0:T(8,128)(2,1)S(1)}, bf16[32,2048]{1,0:T(8,128)(2,1)S(1)}, u32[]{:S(2)}, u32[]{:S(2)}) collective-permute-start(bf16[32,2048]{1,0:T(8,128)(2,1)S(1)} %get-tuple-element.15), channel_id=1, source_target_pairs={{0,4},{4,0},{8,12},{12,8},{16,20},{20,16},{24,28},{28,24},{1,5},{5... | collective-permute-start | bytes 393224 | tf_op jit(solution)/shard_map/ppermute | solution.py:332
  1.6 11.8 %collective-permute-start.3 = (bf16[32,2048]{1,0:T(8,128)(2,1)S(1)}, bf16[32,2048]{1,0:T(8,128)(2,1)S(1)}, u32[]{:S(2)}, u32[]{:S(2)}) collective-permute-start(bf16[32,2048]{1,0:T(8,128)(2,1)S(1)} %get-tuple-element.16), channel_id=1, source_target_pairs={{4,8},{8,4},{12,16},{16,12},{20,24},{24,20},{5,9},{9,5},{13,17},{1... | collective-permute-start | bytes 393224 | tf_op jit(solution)/shard_map/ppermute | solution.py:329
  6.5 1.3 %collective-permute-start = (bf16[16,2048]{1,0:T(8,128)(2,1)S(1)}, bf16[16,2048]{1,0:T(8,128)(2,1)S(1)}, u32[]{:S(2)}, u32[]{:S(2)}) collective-permute-start(bf16[16,2048]{1,0:T(8,128)(2,1)S(1)} %get-tuple-element.13), channel_id=1, source_target_pairs={{0,1},{1,0},{2,3},{3,2},{4,5},{5,4},{6,7},{7,6},{8,9},{9,8},{10,11... | collective-permute-start | bytes 196616 | tf_op jit(solution)/shard_map/ppermute | solution.py:331
  6.6 1.2 %collective-permute-start.1 = (bf16[16,2048]{1,0:T(8,128)(2,1)S(1)}, bf16[16,2048]{1,0:T(8,128)(2,1)S(1)}, u32[]{:S(2)}, u32[]{:S(2)}) collective-permute-start(bf16[16,2048]{1,0:T(8,128)(2,1)S(1)} %get-tuple-element.14), channel_id=1, source_target_pairs={{1,2},{2,1},{5,6},{6,5},{9,10},{10,9},{13,14},{14,13},{17,18},{18,... | collective-permute-start | bytes 196616 | tf_op jit(solution)/shard_map/ppermute | solution.py:330
  14.3 6.1 %collective-permute-start.4 = (f32[8,4,16,128]{3,2,1,0:T(8,128)S(1)}, f32[8,4,16,128]{3,2,1,0:T(8,128)S(1)}, u32[]{:S(2)}, u32[]{:S(2)}) collective-permute-start(f32[8,4,16,128]{3,2,1,0:T(8,128)S(1)} %get-tuple-element.18), channel_id=1, source_target_pairs={{0,1},{1,0},{2,3},{3,2},{4,5},{5,4},{6,7},{7,6},{8,9},{9,8},{10,11... | collective-permute-start | bytes 786440 | tf_op jit(solution)/shard_map/ppermute | solution.py:336
  20.4 5.8 %collective-permute-start.5 = (f32[4,4,16,128]{3,2,1,0:T(8,128)S(1)}, f32[4,4,16,128]{3,2,1,0:T(8,128)S(1)}, u32[]{:S(2)}, u32[]{:S(2)}) collective-permute-start(f32[4,4,16,128]{3,2,1,0:T(8,128)S(1)} %get-tuple-element.20), channel_id=1, source_target_pairs={{0,2},{1,3},{2,0},{3,1},{4,6},{5,7},{6,4},{7,5},{8,10},{9,11},{10,... | collective-permute-start | bytes 393224 | tf_op jit(solution)/shard_map/ppermute | solution.py:336

commit v3 on v2

--- a/solution.py
+++ b/solution.py
@@ -26,11 +26,23 @@
     return lax.rem(lax.axis_index(axis), 2)
 
 
-def pairs(axis, odd):
+def exchange(x, axis, odd):
+    tiles, depths = lax.axis_size("tile"), lax.axis_size("depth")
     found = []
-    for low in range(odd, lax.axis_size(axis) - 1, 2):
-        found += [(low, low + 1), (low + 1, low)]
-    return found
+    for tile in range(tiles):
+        for depth in range(depths):
+            if axis == "tile":
+                other = (tile - odd ^ 1) + odd
+                partner = (other, depth) if 0 <= other < tiles else (tile, depth ^ 1)
+            else:
+                partner = (tile, ((depth - odd ^ 1) + odd) % depths)
+            found.append((tile * depths + depth, partner[0] * depths + partner[1]))
+    return lax.ppermute(x, ("tile", "depth"), found)
+
+
+def inside(axis):
+    index = lax.axis_index(axis)
+    return jnp.where((index == 0) | (index == lax.axis_size(axis) - 1), 0.0, 1.0)
 
 
 def faces_kernel(volume, tile_a, tile_b, depth_a, depth_b, near, far, wide, sems):
@@ -115,8 +127,10 @@
         self.ref[pl.ds(0, self.pitch), :] = blank
         self.ref[pl.ds((self.chunks + 1) * self.pitch, self.pitch), :] = blank
 
-    def put_column(self, slot, block):
+    def put_column(self, slot, block, mask=None):
         wide = block.astype(jnp.float32)
+        if mask is not None:
+            wide = wide * mask
         for c in range(self.chunks):
             lanes = slice(c * LANES, (c + 1) * LANES)
             self.ref[pl.ds(self.row(c, slot, 0), self.cells_z), :] = wide[:, lanes]
@@ -186,7 +200,7 @@
     field = Field(scratch, cells_z, rows_y, cells_x)
     odd_depth = parity("depth")
     field.clear_ends()
-    layers = [depth_a[...].astype(jnp.float32), depth_b[...].astype(jnp.float32)]
+    layers = [depth_a[...].astype(jnp.float32), depth_b[...].astype(jnp.float32) * inside("depth")]
     for layer, other in zip(layers, (odd_depth, 1 - odd_depth)):
         z = cells_z - other * (cells_z + 1)
         for x in range(0, cells_x, SUB):
@@ -224,11 +238,11 @@
     field.clear_ends()
     for slot, x in ((1, 0), (2, 1), (3, cells_x - 2), (4, cells_x - 1)):
         field.put_column(slot, volume[x])
-    for block, other in ((tile_a, odd_tile), (tile_b, 1 - odd_tile)):
-        field.put_column(5 * (1 - other), block[...])
-    for block, other in ((depth_a, odd_depth), (depth_b, 1 - odd_depth)):
+    for block, other, mask in ((tile_a, odd_tile, None), (tile_b, 1 - odd_tile, inside("tile"))):
+        field.put_column(5 * (1 - other), block[...], mask)
+    for block, other, mask in ((depth_a, odd_depth, 1.0), (depth_b, 1 - odd_depth, inside("depth"))):
         z = cells_z - other * (cells_z + 1)
-        layer = block[...].astype(jnp.float32)
+        layer = block[...].astype(jnp.float32) * mask
         field.put_layer(1, z, layer[:1])
         field.put_layer(4, z, layer[cells_x - 1 :])
 
@@ -326,10 +340,10 @@
     pieces = volume.shape[0] // depth_count
     levels = depth_count.bit_length() - 1
     tile_a, tile_b, depth_a, depth_b = faces(volume)
-    tile_b = lax.ppermute(tile_b, "tile", pairs("tile", 1))
-    depth_b = lax.ppermute(depth_b, "depth", pairs("depth", 1))
-    depth_a = lax.ppermute(depth_a, "depth", pairs("depth", 0))
-    tile_a = lax.ppermute(tile_a, "tile", pairs("tile", 0))
+    tile_b = exchange(tile_b, "tile", 1)
+    depth_b = exchange(depth_b, "depth", 1)
+    depth_a = exchange(depth_a, "depth", 0)
+    tile_a = exchange(tile_a, "tile", 0)
     done = inner(volume, depth_a, depth_b, depth_total)
     kept, given = outer(volume, depth_a, depth_b, tile_a, tile_b, done, depth_total)
     for section in range(levels):

time: 27.1 us -> 23.9 us (0.88); the launches traced: 27 us -> 23.4 us
  starting transfers between devices: 12.1 us -> 7.13 us
  waiting for transfers between devices: 6.13 us -> 7.55 us
    ppermute x2, starting transfers between devices: 6.33 us -> 2.43 us  [shards(): lax.ppermute(given, 'depth', [(i, i ^ 1 << section) for i in range(depth_...]
    ppermute x4, waiting for transfers between devices: 0.58 us -> 2.1 us  [exchange(): return lax.ppermute(x, ('tile', 'depth'), found)]
    ppermute x4, starting transfers between devices: 5.73 us -> 4.7 us  [exchange(): return lax.ppermute(x, ('tile', 'depth'), found)]
  transfers between devices with their start and end apart: 6 -> 6, of which waited for: 3 -> 3; matrix products, arithmetic and copies ran while one was open for 0% -> 0% of each run, Pallas kernels for 20% -> 24%
where the time goes in v3:
time: 23.9 us; the launch traced here: 23.4 us
  Pallas kernels  8.68 us (36%)
  waiting for transfers between devices  7.55 us (32%)
  starting transfers between devices  7.13 us (30%)
    pallas_call x1, Pallas kernels, inner(): pl.pallas_call(lambda *refs: inner_kernel(depth_total, *refs), out_shape=...  5.53 us
    ppermute x2, waiting for transfers between devices, shards(): lax.ppermute(given, 'depth', [(i, i ^ 1 << section) for i in range(depth_...  5.45 us
    ppermute x4, starting transfers between devices, exchange(): return lax.ppermute(x, ('tile', 'depth'), found)  4.7 us
    ppermute x2, starting transfers between devices, shards(): lax.ppermute(given, 'depth', [(i, i ^ 1 << section) for i in range(depth_...  2.43 us
    ppermute x4, waiting for transfers between devices, exchange(): return lax.ppermute(x, ('tile', 'depth'), found)  2.1 us
    pallas_call x1, Pallas kernels, faces(): pl.pallas_call(faces_kernel, out_shape=(column, column, layer, layer), in...  1.48 us
    pallas_call x1, Pallas kernels, outer(): pl.pallas_call(lambda *refs: outer_kernel(depth_total, *refs), out_shape=...  0.91 us
    pallas_call x1, Pallas kernels, finish(): pl.pallas_call(lambda section_kept, section_other, image: finish_kernel(s...  0.73 us
  transfers between devices with their start and end apart: 6, of which 3 were waited for; matrix products, arithmetic and copies ran while one was open for 0% of the time, Pallas kernels for 24%

profile of v3, /device:TPU:4, one launch (start us, length us, event | category | flops | bytes accessed | tf_op | source)
XLA Modules:
  0.0 23.4 jit_solution(853848036081915273)
XLA Ops:
  0.0 0.0 copy-start
  0.0 1.5 %faces.1 = (bf16[32,2048]{1,0:T(8,128)(2,1)S(1)}, bf16[32,2048]{1,0:T(8,128)(2,1)S(1)}, bf16[16,2048]{1,0:T(8,128)(2,1)S(1)}, bf16[16,2048]{1,0:T(8,128)(2,1)S(1)}) custom-call(bf16[16,32,2048]{2,1,0:T(8,128)(2,1)} %refs_0_.3), custom_call_target="tpu_custom_call" | custom-call | tf_op jit(solution)/shard_map/faces/pallas_call | solution.py:90
  1.5 0.1 collective-permute-start.2
  1.6 3.0 %collective-permute-start.3 = (bf16[32,2048]{1,0:T(8,128)(2,1)S(1)}, bf16[32,2048]{1,0:T(8,128)(2,1)S(1)}, u32[]{:S(2)}, u32[]{:S(2)}) collective-permute-start(bf16[32,2048]{1,0:T(8,128)(2,1)S(1)} %get-tuple-element.16), channel_id=1, source_target_pairs={{0,1},{1,0},{2,3},{3,2},{4,8},{5,9},{6,10},{7,11},{8,4},{9,5},{10,... | collective-permute-start | bytes 393224 | tf_op jit(solution)/shard_map/ppermute | solution.py:40
  4.6 0.0 collective-permute-start
  4.6 1.6 %collective-permute-start.1 = (bf16[16,2048]{1,0:T(8,128)(2,1)S(1)}, bf16[16,2048]{1,0:T(8,128)(2,1)S(1)}, u32[]{:S(2)}, u32[]{:S(2)}) collective-permute-start(bf16[16,2048]{1,0:T(8,128)(2,1)S(1)} %get-tuple-element.14), channel_id=1, source_target_pairs={{0,3},{1,2},{2,1},{3,0},{4,7},{5,6},{6,5},{7,4},{8,11},{9,10},{10,... | collective-permute-start | bytes 196616 | tf_op jit(solution)/shard_map/ppermute | solution.py:40
  6.2 0.0 collective-permute-done.refs_1_
  6.2 2.1 %collective-permute-done.1.refs_2_ = bf16[16,2048]{1,0:T(8,128)(2,1)S(1)} collective-permute-done((bf16[16,2048]{1,0:T(8,128)(2,1)S(1)}, bf16[16,2048]{1,0:T(8,128)(2,1)S(1)}, u32[]{:S(2)}, u32[]{:S(2)}) %collective-permute-start.1) | collective-permute-done | bytes 65568 | tf_op jit(solution)/shard_map/ppermute | solution.py:40
  8.3 0.0 copy-done
  8.3 5.5 %inner.1.refs_5_ = f32[14,4,16,128]{3,2,1,0:T(8,128)S(1)} custom-call(bf16[16,32,2048]{2,1,0:T(8,128)(2,1)S(1)} %copy-done, bf16[16,2048]{1,0:T(8,128)(2,1)S(1)} %collective-permute-done.refs_1_, bf16[16,2048]{1,0:T(8,128)(2,1)S(1)} %collective-permute-done.1.refs_2_), custom_call_target="tpu_custom_call" | custom-call | flops 100000000 | bytes 10000000 | tf_op jit(solution)/shard_map/inner/pallas_call | solution.py:222
  13.8 0.0 collective-permute-done.2.refs_3_
  13.8 0.0 collective-permute-done.3.refs_4_
  13.9 0.9 %outer.1 = (f32[8,4,16,128]{3,2,1,0:T(8,128)S(1)}, f32[8,4,16,128]{3,2,1,0:T(8,128)S(1)}) custom-call(bf16[16,32,2048]{2,1,0:T(8,128)(2,1)S(1)} %copy-done, bf16[16,2048]{1,0:T(8,128)(2,1)S(1)} %collective-permute-done.refs_1_, bf16[16,2048]{1,0:T(8,128)(2,1)S(1)} %collective-permute-done.1.refs_2_, bf16[32,2048]{1,0:T(8,128)(2,1)S(1)} %collective-permute-done.2.refs_3_, ...), custom_call_target="tpu_custom_call" | custom-call | flops 10000000 | bytes 1000000 | tf_op jit(solution)/shard_map/outer/pallas_call | solution.py:270
  14.8 0.9 %collective-permute-start.4 = (f32[8,4,16,128]{3,2,1,0:T(8,128)S(1)}, f32[8,4,16,128]{3,2,1,0:T(8,128)S(1)}, u32[]{:S(2)}, u32[]{:S(2)}) collective-permute-start(f32[8,4,16,128]{3,2,1,0:T(8,128)S(1)} %get-tuple-element.18), channel_id=1, source_target_pairs={{0,1},{1,0},{2,3},{3,2},{4,5},{5,4},{6,7},{7,6},{8,9},{9,8},{10,11... | collective-permute-start | bytes 786440 | tf_op jit(solution)/shard_map/ppermute | solution.py:350
  15.6 1.2 %collective-permute-done.4.refs_1_ = f32[8,4,16,128]{3,2,1,0:T(8,128)S(1)} collective-permute-done((f32[8,4,16,128]{3,2,1,0:T(8,128)S(1)}, f32[8,4,16,128]{3,2,1,0:T(8,128)S(1)}, u32[]{:S(2)}, u32[]{:S(2)}) %collective-permute-start.4) | collective-permute-done | bytes 262176 | tf_op jit(solution)/shard_map/ppermute | solution.py:350
  16.9 1.6 %collective-permute-start.5 = (f32[4,4,16,128]{3,2,1,0:T(8,128)S(1)}, f32[4,4,16,128]{3,2,1,0:T(8,128)S(1)}, u32[]{:S(2)}, u32[]{:S(2)}) collective-permute-start(f32[4,4,16,128]{3,2,1,0:T(8,128)S(1)} %get-tuple-element.20), channel_id=1, source_target_pairs={{0,2},{1,3},{2,0},{3,1},{4,6},{5,7},{6,4},{7,5},{8,10},{9,11},{10,... | collective-permute-start | bytes 393224 | tf_op jit(solution)/shard_map/ppermute | solution.py:350
  18.4 4.3 %collective-permute-done.5.section_other = f32[4,4,16,128]{3,2,1,0:T(8,128)S(1)} collective-permute-done((f32[4,4,16,128]{3,2,1,0:T(8,128)S(1)}, f32[4,4,16,128]{3,2,1,0:T(8,128)S(1)}, u32[]{:S(2)}, u32[]{:S(2)}) %collective-permute-start.5) | collective-permute-done | bytes 131104 | tf_op jit(solution)/shard_map/ppermute | solution.py:350
  22.7 0.7 %finish.1 = f32[4,4,2048]{2,1,0:T(4,128)} custom-call(f32[4,4,16,128]{3,2,1,0:T(8,128)S(1)} %get-tuple-element.19.section_kept, f32[4,4,16,128]{3,2,1,0:T(8,128)S(1)} %collective-permute-done.5.section_other), custom_call_target="tpu_custom_call" | custom-call | tf_op jit(solution)/shard_map/finish/pallas_call | solution.py:327
  (1 shorter events, 0.0 us)
Async XLA Ops:
  0.0 8.3 %copy-start = (bf16[16,32,2048]{2,1,0:T(8,128)(2,1)S(1)}, bf16[16,32,2048]{2,1,0:T(8,128)(2,1)}, u32[]{:S(2)}) copy-start(bf16[16,32,2048]{2,1,0:T(8,128)(2,1)} %refs_0_.3) | copy-start | bytes 6291460
  1.5 12.4 %collective-permute-start.2 = (bf16[32,2048]{1,0:T(8,128)(2,1)S(1)}, bf16[32,2048]{1,0:T(8,128)(2,1)S(1)}, u32[]{:S(2)}, u32[]{:S(2)}) collective-permute-start(bf16[32,2048]{1,0:T(8,128)(2,1)S(1)} %get-tuple-element.15), channel_id=1, source_target_pairs={{0,4},{1,5},{2,6},{3,7},{4,0},{5,1},{6,2},{7,3},{8,12},{9,13},{10,... | collective-permute-start | bytes 393224 | tf_op jit(solution)/shard_map/ppermute | solution.py:40
  1.6 12.3 %collective-permute-start.3 = (bf16[32,2048]{1,0:T(8,128)(2,1)S(1)}, bf16[32,2048]{1,0:T(8,128)(2,1)S(1)}, u32[]{:S(2)}, u32[]{:S(2)}) collective-permute-start(bf16[32,2048]{1,0:T(8,128)(2,1)S(1)} %get-tuple-element.16), channel_id=1, source_target_pairs={{0,1},{1,0},{2,3},{3,2},{4,8},{5,9},{6,10},{7,11},{8,4},{9,5},{10,... | collective-permute-start | bytes 393224 | tf_op jit(solution)/shard_map/ppermute | solution.py:40
  4.6 1.6 %collective-permute-start = (bf16[16,2048]{1,0:T(8,128)(2,1)S(1)}, bf16[16,2048]{1,0:T(8,128)(2,1)S(1)}, u32[]{:S(2)}, u32[]{:S(2)}) collective-permute-start(bf16[16,2048]{1,0:T(8,128)(2,1)S(1)} %get-tuple-element.13), channel_id=1, source_target_pairs={{0,1},{1,0},{2,3},{3,2},{4,5},{5,4},{6,7},{7,6},{8,9},{9,8},{10,11... | collective-permute-start | bytes 196616 | tf_op jit(solution)/shard_map/ppermute | solution.py:40
  4.6 3.7 %collective-permute-start.1 = (bf16[16,2048]{1,0:T(8,128)(2,1)S(1)}, bf16[16,2048]{1,0:T(8,128)(2,1)S(1)}, u32[]{:S(2)}, u32[]{:S(2)}) collective-permute-start(bf16[16,2048]{1,0:T(8,128)(2,1)S(1)} %get-tuple-element.14), channel_id=1, source_target_pairs={{0,3},{1,2},{2,1},{3,0},{4,7},{5,6},{6,5},{7,4},{8,11},{9,10},{10,... | collective-permute-start | bytes 196616 | tf_op jit(solution)/shard_map/ppermute | solution.py:40
  14.8 2.0 %collective-permute-start.4 = (f32[8,4,16,128]{3,2,1,0:T(8,128)S(1)}, f32[8,4,16,128]{3,2,1,0:T(8,128)S(1)}, u32[]{:S(2)}, u32[]{:S(2)}) collective-permute-start(f32[8,4,16,128]{3,2,1,0:T(8,128)S(1)} %get-tuple-element.18), channel_id=1, source_target_pairs={{0,1},{1,0},{2,3},{3,2},{4,5},{5,4},{6,7},{7,6},{8,9},{9,8},{10,11... | collective-permute-start | bytes 786440 | tf_op jit(solution)/shard_map/ppermute | solution.py:350
  16.9 5.8 %collective-permute-start.5 = (f32[4,4,16,128]{3,2,1,0:T(8,128)S(1)}, f32[4,4,16,128]{3,2,1,0:T(8,128)S(1)}, u32[]{:S(2)}, u32[]{:S(2)}) collective-permute-start(f32[4,4,16,128]{3,2,1,0:T(8,128)S(1)} %get-tuple-element.20), channel_id=1, source_target_pairs={{0,2},{1,3},{2,0},{3,1},{4,6},{5,7},{6,4},{7,5},{8,10},{9,11},{10,... | collective-permute-start | bytes 393224 | tf_op jit(solution)/shard_map/ppermute | solution.py:350

commit v4 on v3

--- a/solution.py
+++ b/solution.py
@@ -17,6 +17,8 @@
 LOG2E = math.log2(math.e)
 LANES = 128
 SUB = 8
+POWER = 16.0
+CENTRE = 7.9
 
 VMEM = pl.BlockSpec(memory_space=pltpu.VMEM)
 HBM = pl.BlockSpec(memory_space=pltpu.HBM)
@@ -35,7 +37,8 @@
                 other = (tile - odd ^ 1) + odd
                 partner = (other, depth) if 0 <= other < tiles else (tile, depth ^ 1)
             else:
-                partner = (tile, ((depth - odd ^ 1) + odd) % depths)
+                other = (depth - odd ^ 1) + odd
+                partner = (tile, other) if 0 <= other < depths else (tile ^ 1, depth)
             found.append((tile * depths + depth, partner[0] * depths + partner[1]))
     return lax.ppermute(x, ("tile", "depth"), found)
 
@@ -288,6 +291,23 @@
     return [a + front[3] * b for a, b in zip(front[:3], back[:3])] + [front[3] * back[3]]
 
 
+def encode(channels):
+    red, green, blue, passing = channels
+    return [
+        jnp.exp2(POWER * (jnp.log2(x) + CENTRE)).astype(jnp.bfloat16) for x in (red, green, blue, 1.0 - passing)
+    ]
+
+
+def decode(codes):
+    red, green, blue, opacity = [jnp.exp2(jnp.log2(y.astype(jnp.float32)) * (1.0 / POWER) - CENTRE) for y in codes]
+    return [red, green, blue, 1.0 - opacity]
+
+
+def received(block):
+    channels = [block[channel] for channel in range(4)]
+    return decode(channels) if block.dtype == jnp.bfloat16 else channels
+
+
 def merge_kernel(section, pieces, kept, other, next_kept, next_given):
     position = lax.axis_index("depth")
     in_front = lax.rem(position // 2**section, 2) == 0
@@ -295,15 +315,16 @@
     for i in range(kept.shape[0] // 2):
         low = i // pieces * 2 * pieces + i % pieces
         for target, x in ((next_kept, low + upper * pieces), (next_given, low + (1 - upper) * pieces)):
-            for channel, value in enumerate(over(list(kept[x]), list(other[x]), in_front)):
+            channels = over(list(kept[x]), received(other[x]), in_front)
+            for channel, value in enumerate(encode(channels) if target is next_given else channels):
                 target[i, channel] = value
 
 
 def merge(kept, other, section, pieces):
-    half = jax.ShapeDtypeStruct((kept.shape[0] // 2, *kept.shape[1:]), kept.dtype)
+    shape = (kept.shape[0] // 2, *kept.shape[1:])
     return pl.pallas_call(
         lambda *refs: merge_kernel(section, pieces, *refs),
-        out_shape=(half, half),
+        out_shape=(jax.ShapeDtypeStruct(shape, jnp.float32), jax.ShapeDtypeStruct(shape, jnp.bfloat16)),
         in_specs=[VMEM] * 2,
         out_specs=(VMEM, VMEM),
         compiler_params=pltpu.CompilerParams(vmem_limit_bytes=8 << 20),
@@ -316,7 +337,7 @@
     in_front = lax.rem(position // 2**section, 2) == 0
     columns, _, chunks, _ = kept.shape
     for x in range(columns):
-        red, green, blue, passing = over(list(kept[x]), list(other[x]), in_front)
+        red, green, blue, passing = over(list(kept[x]), received(other[x]), in_front)
         for channel, value in enumerate((red, green, blue, 1.0 - passing)):
             for c in range(chunks):
                 image[channel, pl.ds(x, 1), pl.ds(c * LANES, LANES)] = value[c : c + 1]

time: 23.9 us -> 24.2 us (1.013)
  the two profiles are of different devices: /device:TPU:4 before, /device:TPU:0 now
where the time goes in v4:
time: 24.2 us; the launch traced here: 24.1 us
  Pallas kernels  8.74 us (36%)
  waiting for transfers between devices  8.21 us (34%)
  starting transfers between devices  7.04 us (29%)
    ppermute x4, starting transfers between devices, exchange(): return lax.ppermute(x, ('tile', 'depth'), found)  6.1 us
    pallas_call x1, Pallas kernels, inner(): pl.pallas_call(lambda *refs: inner_kernel(depth_total, *refs), out_shape=...  5.53 us
    ppermute x2, waiting for transfers between devices, shards(): lax.ppermute(given, 'depth', [(i, i ^ 1 << section) for i in range(depth_...  4.98 us
    ppermute x4, waiting for transfers between devices, exchange(): return lax.ppermute(x, ('tile', 'depth'), found)  3.23 us
    pallas_call x1, Pallas kernels, faces(): pl.pallas_call(faces_kernel, out_shape=(column, column, layer, layer), in...  1.48 us
    ppermute x2, starting transfers between devices, shards(): lax.ppermute(given, 'depth', [(i, i ^ 1 << section) for i in range(depth_...  0.94 us
    pallas_call x1, Pallas kernels, outer(): pl.pallas_call(lambda *refs: outer_kernel(depth_total, *refs), out_shape=...  0.91 us
    pallas_call x1, Pallas kernels, finish(): pl.pallas_call(lambda section_kept, section_other, image: finish_kernel(s...  0.76 us
  transfers between devices with their start and end apart: 6, of which 3 were waited for; matrix products, arithmetic and copies ran while one was open for 0% of the time, Pallas kernels for 23%

profile of v4, /device:TPU:0, one launch (start us, length us, event | category | flops | bytes accessed | tf_op | source)
XLA Modules:
  0.0 24.1 jit_solution(6120017735598970192)
XLA Ops:
  0.0 0.0 copy-start
  0.0 1.5 %faces.1 = (bf16[32,2048]{1,0:T(8,128)(2,1)S(1)}, bf16[32,2048]{1,0:T(8,128)(2,1)S(1)}, bf16[16,2048]{1,0:T(8,128)(2,1)S(1)}, bf16[16,2048]{1,0:T(8,128)(2,1)S(1)}) custom-call(bf16[16,32,2048]{2,1,0:T(8,128)(2,1)} %refs_0_.3), custom_call_target="tpu_custom_call" | custom-call | tf_op jit(solution)/shard_map/faces/pallas_call | solution.py:93
  1.5 3.1 %collective-permute-start.2 = (bf16[32,2048]{1,0:T(8,128)(2,1)S(1)}, bf16[32,2048]{1,0:T(8,128)(2,1)S(1)}, u32[]{:S(2)}, u32[]{:S(2)}) collective-permute-start(bf16[32,2048]{1,0:T(8,128)(2,1)S(1)} %get-tuple-element.15), channel_id=1, source_target_pairs={{0,4},{1,5},{2,6},{3,7},{4,0},{5,1},{6,2},{7,3},{8,12},{9,13},{10,... | collective-permute-start | bytes 393224 | tf_op jit(solution)/shard_map/ppermute | solution.py:43
  4.5 0.0 collective-permute-start.3
  4.6 0.5 %collective-permute-start = (bf16[16,2048]{1,0:T(8,128)(2,1)S(1)}, bf16[16,2048]{1,0:T(8,128)(2,1)S(1)}, u32[]{:S(2)}, u32[]{:S(2)}) collective-permute-start(bf16[16,2048]{1,0:T(8,128)(2,1)S(1)} %get-tuple-element.13), channel_id=1, source_target_pairs={{0,1},{1,0},{2,3},{3,2},{4,5},{5,4},{6,7},{7,6},{8,9},{9,8},{10,11... | collective-permute-start | bytes 196616 | tf_op jit(solution)/shard_map/ppermute | solution.py:43
  5.1 2.5 %collective-permute-start.1 = (bf16[16,2048]{1,0:T(8,128)(2,1)S(1)}, bf16[16,2048]{1,0:T(8,128)(2,1)S(1)}, u32[]{:S(2)}, u32[]{:S(2)}) collective-permute-start(bf16[16,2048]{1,0:T(8,128)(2,1)S(1)} %get-tuple-element.14), channel_id=1, source_target_pairs={{0,4},{1,2},{2,1},{3,7},{4,0},{5,6},{6,5},{7,3},{8,12},{9,10},{10,... | collective-permute-start | bytes 196616 | tf_op jit(solution)/shard_map/ppermute | solution.py:43
  7.6 0.0 collective-permute-done.refs_1_
  7.6 3.2 %collective-permute-done.1.refs_2_ = bf16[16,2048]{1,0:T(8,128)(2,1)S(1)} collective-permute-done((bf16[16,2048]{1,0:T(8,128)(2,1)S(1)}, bf16[16,2048]{1,0:T(8,128)(2,1)S(1)}, u32[]{:S(2)}, u32[]{:S(2)}) %collective-permute-start.1) | collective-permute-done | bytes 65568 | tf_op jit(solution)/shard_map/ppermute | solution.py:43
  10.8 0.0 copy-done
  10.8 5.5 %inner.1.refs_5_ = f32[14,4,16,128]{3,2,1,0:T(8,128)S(1)} custom-call(bf16[16,32,2048]{2,1,0:T(8,128)(2,1)S(1)} %copy-done, bf16[16,2048]{1,0:T(8,128)(2,1)S(1)} %collective-permute-done.refs_1_, bf16[16,2048]{1,0:T(8,128)(2,1)S(1)} %collective-permute-done.1.refs_2_), custom_call_target="tpu_custom_call" | custom-call | flops 100000000 | bytes 10000000 | tf_op jit(solution)/shard_map/inner/pallas_call | solution.py:225
  16.4 0.0 collective-permute-done.2.refs_3_
  16.4 0.0 collective-permute-done.3.refs_4_
  16.4 0.9 %outer.1 = (f32[8,4,16,128]{3,2,1,0:T(8,128)S(1)}, f32[8,4,16,128]{3,2,1,0:T(8,128)S(1)}) custom-call(bf16[16,32,2048]{2,1,0:T(8,128)(2,1)S(1)} %copy-done, bf16[16,2048]{1,0:T(8,128)(2,1)S(1)} %collective-permute-done.refs_1_, bf16[16,2048]{1,0:T(8,128)(2,1)S(1)} %collective-permute-done.1.refs_2_, bf16[32,2048]{1,0:T(8,128)(2,1)S(1)} %collective-permute-done.2.refs_3_, ...), custom_call_target="tpu_custom_call" | custom-call | flops 10000000 | bytes 1000000 | tf_op jit(solution)/shard_map/outer/pallas_call | solution.py:273
  17.3 0.1 collective-permute-start.4
  17.4 1.5 %collective-permute-done.4.refs_1_ = f32[8,4,16,128]{3,2,1,0:T(8,128)S(1)} collective-permute-done((f32[8,4,16,128]{3,2,1,0:T(8,128)S(1)}, f32[8,4,16,128]{3,2,1,0:T(8,128)S(1)}, u32[]{:S(2)}, u32[]{:S(2)}) %collective-permute-start.4) | collective-permute-done | bytes 262176 | tf_op jit(solution)/shard_map/ppermute | solution.py:371
  18.9 0.1 merge.1
  19.0 0.9 %collective-permute-start.5 = (bf16[4,4,16,128]{3,2,1,0:T(8,128)(2,1)S(1)}, bf16[4,4,16,128]{3,2,1,0:T(8,128)(2,1)S(1)}, u32[]{:S(2)}, u32[]{:S(2)}) collective-permute-start(bf16[4,4,16,128]{3,2,1,0:T(8,128)(2,1)S(1)} %get-tuple-element.20), channel_id=1, source_target_pairs={{0,2},{1,3},{2,0},{3,1},{4,6},{5,7},{6,4},{7,5},{8,10},{9,11},{10,... | collective-permute-start | bytes 196616 | tf_op jit(solution)/shard_map/ppermute | solution.py:371
  19.8 3.5 %collective-permute-done.5.section_other = bf16[4,4,16,128]{3,2,1,0:T(8,128)(2,1)S(1)} collective-permute-done((bf16[4,4,16,128]{3,2,1,0:T(8,128)(2,1)S(1)}, bf16[4,4,16,128]{3,2,1,0:T(8,128)(2,1)S(1)}, u32[]{:S(2)}, u32[]{:S(2)}) %collective-permute-start.5) | collective-permute-done | bytes 65568 | tf_op jit(solution)/shard_map/ppermute | solution.py:371
  23.3 0.8 %finish.1 = f32[4,4,2048]{2,1,0:T(4,128)} custom-call(f32[4,4,16,128]{3,2,1,0:T(8,128)S(1)} %get-tuple-element.19.section_kept, bf16[4,4,16,128]{3,2,1,0:T(8,128)(2,1)S(1)} %collective-permute-done.5.section_other), custom_call_target="tpu_custom_call" | custom-call | tf_op jit(solution)/shard_map/finish/pallas_call | solution.py:348
Async XLA Ops:
  0.0 10.8 %copy-start = (bf16[16,32,2048]{2,1,0:T(8,128)(2,1)S(1)}, bf16[16,32,2048]{2,1,0:T(8,128)(2,1)}, u32[]{:S(2)}) copy-start(bf16[16,32,2048]{2,1,0:T(8,128)(2,1)} %refs_0_.3) | copy-start | bytes 6291460
  1.5 14.9 %collective-permute-start.2 = (bf16[32,2048]{1,0:T(8,128)(2,1)S(1)}, bf16[32,2048]{1,0:T(8,128)(2,1)S(1)}, u32[]{:S(2)}, u32[]{:S(2)}) collective-permute-start(bf16[32,2048]{1,0:T(8,128)(2,1)S(1)} %get-tuple-element.15), channel_id=1, source_target_pairs={{0,4},{1,5},{2,6},{3,7},{4,0},{5,1},{6,2},{7,3},{8,12},{9,13},{10,... | collective-permute-start | bytes 393224 | tf_op jit(solution)/shard_map/ppermute | solution.py:43
  4.5 11.8 %collective-permute-start.3 = (bf16[32,2048]{1,0:T(8,128)(2,1)S(1)}, bf16[32,2048]{1,0:T(8,128)(2,1)S(1)}, u32[]{:S(2)}, u32[]{:S(2)}) collective-permute-start(bf16[32,2048]{1,0:T(8,128)(2,1)S(1)} %get-tuple-element.16), channel_id=1, source_target_pairs={{0,1},{1,0},{2,3},{3,2},{4,8},{5,9},{6,10},{7,11},{8,4},{9,5},{10,... | collective-permute-start | bytes 393224 | tf_op jit(solution)/shard_map/ppermute | solution.py:43
  4.6 3.0 %collective-permute-start = (bf16[16,2048]{1,0:T(8,128)(2,1)S(1)}, bf16[16,2048]{1,0:T(8,128)(2,1)S(1)}, u32[]{:S(2)}, u32[]{:S(2)}) collective-permute-start(bf16[16,2048]{1,0:T(8,128)(2,1)S(1)} %get-tuple-element.13), channel_id=1, source_target_pairs={{0,1},{1,0},{2,3},{3,2},{4,5},{5,4},{6,7},{7,6},{8,9},{9,8},{10,11... | collective-permute-start | bytes 196616 | tf_op jit(solution)/shard_map/ppermute | solution.py:43
  5.1 5.8 %collective-permute-start.1 = (bf16[16,2048]{1,0:T(8,128)(2,1)S(1)}, bf16[16,2048]{1,0:T(8,128)(2,1)S(1)}, u32[]{:S(2)}, u32[]{:S(2)}) collective-permute-start(bf16[16,2048]{1,0:T(8,128)(2,1)S(1)} %get-tuple-element.14), channel_id=1, source_target_pairs={{0,4},{1,2},{2,1},{3,7},{4,0},{5,6},{6,5},{7,3},{8,12},{9,10},{10,... | collective-permute-start | bytes 196616 | tf_op jit(solution)/shard_map/ppermute | solution.py:43
  17.3 1.6 %collective-permute-start.4 = (f32[8,4,16,128]{3,2,1,0:T(8,128)S(1)}, f32[8,4,16,128]{3,2,1,0:T(8,128)S(1)}, u32[]{:S(2)}, u32[]{:S(2)}) collective-permute-start(f32[8,4,16,128]{3,2,1,0:T(8,128)S(1)} %get-tuple-element.18), channel_id=1, source_target_pairs={{0,1},{1,0},{2,3},{3,2},{4,5},{5,4},{6,7},{7,6},{8,9},{9,8},{10,11... | collective-permute-start | bytes 786440 | tf_op jit(solution)/shard_map/ppermute | solution.py:371
  19.0 4.3 %collective-permute-start.5 = (bf16[4,4,16,128]{3,2,1,0:T(8,128)(2,1)S(1)}, bf16[4,4,16,128]{3,2,1,0:T(8,128)(2,1)S(1)}, u32[]{:S(2)}, u32[]{:S(2)}) collective-permute-start(bf16[4,4,16,128]{3,2,1,0:T(8,128)(2,1)S(1)} %get-tuple-element.20), channel_id=1, source_target_pairs={{0,2},{1,3},{2,0},{3,1},{4,6},{5,7},{6,4},{7,5},{8,10},{9,11},{10,... | collective-permute-start | bytes 196616 | tf_op jit(solution)/shard_map/ppermute | solution.py:371
